TPU v7x, 32 devices: a whole 2x2x4 slice. The times are simulated.
32 devices in a mesh: series: 4 (over z), head: 8 (over y, x, core).
Axes of the slice: x: 2, y: 2, z: 4, core: 2. Of those that a mesh axis runs over, the one named last changes fastest.
Arguments:
- teacher_in: bfloat16 [32, 128, 4096], P(('series', 'head')), may hold values from -6 to 6
- teacher_gain: float32 [4096], replicated, may hold values from 0.5 to 1.5
- w_gate: bfloat16 [4096, 8192], P(None, 'head'), may hold values from -0.09375 to 0.09375
- w_up: bfloat16 [4096, 8192], P(None, 'head'), may hold values from -0.09375 to 0.09375
- readout: bfloat16 [8192, 1024], P('head'), may hold values from -0.0625 to 0.0625
- distill_proj: bfloat16 [4096, 1024], P('head'), may hold values from -0.09375 to 0.09375
- building_ids: int32 [32], P(('series', 'head')), may hold values from 0 to 1023
- student_in: bfloat16 [32, 128, 1024], P(('series', 'head')), may hold values from -6 to 6
- embed_rows: bfloat16 [1024, 1024], replicated, may hold values from -4 to 4
- covariates: bfloat16 [1024, 128], replicated, may hold values from -5 to 5
- cov_proj: bfloat16 [128, 1024], replicated, may hold values from -0.5 to 0.5
- student_gain: float32 [1024], replicated, may hold values from 0.25 to 1.75
- w_x: bfloat16 [1024, 2048], replicated, may hold values from -0.1875 to 0.1875
- w_bcdt: bfloat16 [1024, 288], replicated, may hold values from -0.1875 to 0.1875
- conv_w: float32 [4, 2304], replicated, may hold values from -3 to 3
- dt_bias: float32 [32], replicated, may hold values from -1 to 1
- a_log: float32 [32], replicated, may hold values from -6 to -2.5
- d_skip: float32 [32], replicated, may hold values from 0.5 to 1.5
- norm_gain: float32 [2048], replicated, may hold values from 0.25 to 1.75
- w_out: bfloat16 [2048, 1024], replicated, may hold values from -0.125 to 0.125
Outputs:
- grad_bcdt: float32 [1024, 288], P(('series', 'head'))
- grad_conv: float32 [4, 2304], P(None, ('series', 'head'))
- grad_gain: float32 [2048], P(('series', 'head'))
- grad_out: float32 [2048, 1024], P(('series', 'head'))
Inputs may be any that keep to these rules, and one draw needn't show every extreme that they name: `building_ids`: building ids index rows of the building tables.
All inputs are finite; a program needn't handle non-finite values.
Results may differ from a plain program's by a relative error of at most 0.013.
The roundings to bfloat16 on the way count: a program that leaves them out, or rounds other values in their place, can miss the bound.
Values may be sent and summed in bfloat16 or wider, within the bound.
No kernel may reach another device: no remote copies, remote signals or barrier semaphores. Data moves between devices by JAX's collectives and lax.ppermute only.
A program may use at most 128 MiB of HBM per device.

v0:
```python
import jax
import jax.numpy as jnp
from jax import lax
from jax.experimental import pallas as pl
from jax.experimental.pallas import tpu as pltpu
from jax.sharding import PartitionSpec as P

EPS = 1e-05


VMEM = pl.BlockSpec(memory_space=pltpu.VMEM)
SMEM = pl.BlockSpec(memory_space=pltpu.SMEM)
PAIR = 128
TERM_ROWS = 32
TERM_CHUNKS = 6
LOADS, INPUTS = 5, 12
HEAD, CORE, LEVEL, CHIP, DEVICE = range(5)


def exact_dot(left, right, dims=((1,), (0,))):
    return lax.dot_general(
        left, right, (dims, ((), ())), precision=lax.Precision.HIGHEST,
        preferred_element_type=jnp.float32,
    )


def halves(values):
    high = values.astype(jnp.bfloat16)
    return high, (values - high.astype(jnp.float32)).astype(jnp.bfloat16)


def close_dot(left, right, dims=((1,), (0,))):
    (lh, ll), (rh, rl) = halves(left), halves(right)

    def dot(a, b):
        return lax.dot_general(a, b, (dims, ((), ())), preferred_element_type=jnp.float32)

    return dot(lh, rh) + (dot(lh, rl) + dot(ll, rh))


def delayed(values, rows):
    if rows == 0:
        return values
    at = lax.broadcasted_iota(jnp.int32, values.shape, 0)
    return jnp.where(at >= rows, pltpu.roll(values, rows, 0), 0.0)


def advanced(values, rows):
    if rows == 0:
        return values
    size = values.shape[0]
    at = lax.broadcasted_iota(jnp.int32, values.shape, 0)
    return jnp.where(at < size - rows, pltpu.roll(values, size - rows, 0), 0.0)


def head_lanes(head_count, width):
    head = lax.broadcasted_iota(jnp.int32, (head_count, width), 0)
    lane = lax.broadcasted_iota(jnp.int32, (head_count, width), 1)
    size = width // head_count
    return ((lane >= head * size) & (lane < (head + 1) * size)).astype(jnp.float32)


def stacked_by_head(values, head_size):
    lane = lax.broadcasted_iota(jnp.int32, values.shape, 1)
    return jnp.concatenate(
        [
            jnp.where((lane >= at) & (lane < at + head_size), values, 0.0)
            for at in range(0, values.shape[1], head_size)
        ]
    )


def forward_kernel(
    chips, levels, meta, *refs
):
    far, refs = refs[: INPUTS + LOADS], refs[INPUTS + LOADS :]
    near, refs = list(refs[:LOADS]), refs[LOADS:]
    held, sems, refs = list(refs[-INPUTS - 1 : -1]), refs[-1], refs[: -INPUTS - 1]
    loads = [pltpu.make_async_copy(f, n, sems.at[i]) for i, (f, n) in enumerate(zip(far, held + near))]
    for copy in loads[:INPUTS]:
        copy.start()
    for copy in loads[:INPUTS]:
        copy.wait()
    loads = loads[INPUTS:]
    for copy in loads:
        copy.start()
    x, emb, cov, cov_proj, s_gain, w_x, w_bcdt, conv_w, dt_bias, a_log, d_skip, n_gain = held
    w_out = near[0]
    outgoing = refs[:chips]
    (output, mix, slope, xa, dt_wide, y, inv, decay_t, scores_t, bc, dt, gate_dt,
     normed, rounded, sorted_cols) = refs[chips:]
    f32 = jnp.float32
    seq, inner = xa.shape
    heads = dt.shape[1]
    state = bc.shape[1] // 2
    head_size = inner // heads
    extra = emb[...].astype(f32) + jnp.dot(cov[...], cov_proj[...], preferred_element_type=f32)[:1]
    base = x[...].astype(f32) + extra
    mean_sq = jnp.mean(base * base, axis=-1, keepdims=True)
    normed[...] = (base * lax.rsqrt(mean_sq + EPS) * s_gain[...]).astype(jnp.bfloat16)
    projected = lax.dot_general(
        normed[...], w_bcdt[...], (((1,), (1,)), ((), ())), preferred_element_type=f32
    )
    mix[:, :inner] = jnp.dot(normed[...], w_x[...], preferred_element_type=f32)
    mix[:, inner:] = projected[:, : 2 * state]

    taps = conv_w.shape[0]
    for at in range(0, inner + 2 * state, 256):
        cols = slice(at, at + 256)
        values = mix[:, cols]
        conv = values * conv_w[taps - 1 : taps, cols]
        for k in range(taps - 1):
            conv = conv + delayed(values, taps - 1 - k) * conv_w[k : k + 1, cols]
        gate = 1.0 / (1.0 + jnp.exp(-conv))
        slope[:, cols] = gate * (1.0 + conv * (1.0 - gate))
        if at < inner:
            xa[:, cols] = conv * gate
        else:
            bc[:, at - inner : at - inner + 256] = conv * gate

    logits = projected[:, 2 * state : 2 * state + heads] + dt_bias[...]
    steps = jnp.maximum(logits, 0.0) + jnp.log1p(jnp.exp(-jnp.abs(logits)))
    dt[...] = steps
    gate_dt[...] = 1.0 / (1.0 + jnp.exp(-logits))
    row = lax.broadcasted_iota(jnp.int32, (seq, seq), 0)
    col = lax.broadcasted_iota(jnp.int32, (seq, seq), 1)
    running = exact_dot((row >= col).astype(f32), steps * -jnp.exp(a_log[...]))
    running_t = jnp.concatenate([running, jnp.zeros((seq, 128 - heads), f32)], axis=1).T
    lanes = head_lanes(heads, inner)
    dt_wide[...] = exact_dot(steps, lanes)
    scores = exact_dot(bc[:, state:], bc[:, :state], ((1,), (1,)))
    scores_t[...] = scores.T

    group = PAIR // head_size
    for p in range(inner // PAIR):
        cols = slice(p * PAIR, (p + 1) * PAIR)
        weights = []
        for h in range(p * group, (p + 1) * group):
            down, across = running[:, h : h + 1], running_t[h : h + 1, :]
            decay = jnp.exp(jnp.where(row >= col, down - across, -1e30))
            decay_t[h] = jnp.exp(jnp.where(col >= row, across - down, -1e30))
            weights.append(scores * decay)
        held = stacked_by_head(dt_wide[:, cols] * xa[:, cols], head_size)
        y[:, cols] = close_dot(jnp.concatenate(weights, axis=1), held)

    skip = exact_dot(jnp.broadcast_to(d_skip[...], (8, heads)), lanes)[:1]
    mixed = y[...] + skip * xa[...]
    scale = lax.rsqrt(jnp.mean(mixed * mixed, axis=-1, keepdims=True) + EPS)
    inv[...] = jnp.broadcast_to(scale, inv.shape)
    rounded[...] = (mixed * scale * n_gain[...]).astype(jnp.bfloat16)
    loads[0].wait()
    output[...] = jnp.dot(rounded[...], w_out[...], preferred_element_type=f32)

    start = 0
    for values in (rounded, normed):
        width = values.shape[1] // (levels * chips)
        for z in range(levels):
            for chip in range(chips):
                at = (z * chips + chip) * width
                sorted_cols[chip, :, start : start + width] = values[:, at : at + width]
            start += width
    for k in range(chips):
        outgoing[k][...] = sorted_cols[meta[CHIP] ^ k]
    for copy in loads[1:]:
        copy.wait()


def backward_kernel(
    d_out, w_out, n_gain, conv_w, a_log, d_skip, mix, slope, xa, dt_wide, y, inv, decay_t, scores_t,
    bc, dt, gate_dt, message, g_conv, d_mixed, through,
):
    f32 = jnp.float32
    seq, inner = xa.shape
    heads = dt.shape[1]
    state = bc.shape[1] // 2
    head_size = inner // heads
    taps = conv_w.shape[0]
    lanes = head_lanes(heads, inner)
    skip = exact_dot(jnp.broadcast_to(d_skip[...], (8, heads)), lanes)[:1]
    scale = inv[:, :1]
    d_norm = lax.dot_general(
        d_out[...], w_out[...], (((1,), (1,)), ((), ())), preferred_element_type=f32
    )
    unit = (y[...] + skip * xa[...]) * scale
    wide = message.shape[1]
    bf16 = jnp.bfloat16
    message[...] = jnp.zeros_like(message)
    g_conv[...] = jnp.zeros_like(g_conv)
    g_conv[taps : taps + 1, :inner] = jnp.sum(d_norm * unit, axis=0, keepdims=True)
    pulled = d_norm * n_gain[...]
    d_mixed[...] = scale * (pulled - unit * jnp.mean(pulled * unit, axis=-1, keepdims=True))

    group = PAIR // head_size
    d_scores_t = jnp.zeros((seq, seq), f32)
    scored = scores_t[...]
    for p in range(inner // PAIR):
        cols = slice(p * PAIR, (p + 1) * PAIR)
        got = d_mixed[:, cols]
        held = dt_wide[:, cols] * xa[:, cols]
        weights = jnp.concatenate(
            [scored * decay_t[h] for h in range(p * group, (p + 1) * group)], axis=1
        )
        through[:, cols] = close_dot(weights, stacked_by_head(got, head_size))
        outer = close_dot(stacked_by_head(held, head_size), got, ((1,), (1,)))
        for i in range(group):
            d_scores_t = d_scores_t + outer[i * seq : (i + 1) * seq] * decay_t[p * group + i]

    d_dt = exact_dot(through[...] * xa[...], lanes, ((1,), (1,)))
    d_running = exact_dot(d_mixed[...] * y[...], lanes, ((1,), (1,))) - dt[...] * d_dt
    row = lax.broadcasted_iota(jnp.int32, (seq, seq), 0)
    col = lax.broadcasted_iota(jnp.int32, (seq, seq), 1)
    later = exact_dot((col >= row).astype(f32), d_running)
    d_step = (d_dt + later * -jnp.exp(a_log[...])) * gate_dt[...]

    for at in range(0, inner, 256):
        cols = slice(at, at + 256)
        d_act = dt_wide[:, cols] * through[:, cols] + skip[:, cols] * d_mixed[:, cols]
        d_conv = d_act * slope[:, cols]
        values = mix[:, cols]
        for k in range(taps):
            g_conv[k : k + 1, cols] = jnp.sum(
                d_conv * delayed(values, taps - 1 - k), axis=0, keepdims=True
            )
    d_b = exact_dot(d_scores_t, bc[:, state:])
    d_c = exact_dot(d_scores_t.T, bc[:, :state])
    for at, d_act in ((0, d_b), (state, d_c)):
        cols = slice(inner + at, inner + at + state)
        d_conv = d_act * slope[:, cols]
        values = mix[:, cols]
        d_mix = d_conv * conv_w[taps - 1 : taps, cols]
        for k in range(taps):
            g_conv[k : k + 1, cols] = jnp.sum(
                d_conv * delayed(values, taps - 1 - k), axis=0, keepdims=True
            )
            if k < taps - 1:
                d_mix = d_mix + advanced(d_conv, taps - 1 - k) * conv_w[k : k + 1, cols]
        message[:seq, at : at + state] = d_mix.astype(bf16)
    message[:seq, 2 * state : 2 * state + heads] = d_step.astype(bf16)
    per_row = (inner + 2 * state) // wide
    packed = [
        g_conv[k : k + 1, i * wide : (i + 1) * wide] for k in range(taps + 1) for i in range(per_row)
    ]
    packed = packed + [jnp.zeros_like(packed[0])] * (TERM_ROWS - len(packed))
    message[seq:, :] = jnp.concatenate(packed).astype(bf16)


def cost(micros):
    return pl.CostEstimate(flops=int(micros * 1e9), transcendentals=0, bytes_accessed=0)


def pinned(shape, dtype):
    return pltpu.VMEM(shape, dtype)


def in_vmem(values):
    return [pltpu.with_memory_space_constraint(v, pltpu.VMEM) for v in values]


def student_forward(chips, levels, meta, inputs, loads):
    x, *_, w_x, _, conv_w, dt_bias, _, _, _ = inputs
    seq, width = x.shape
    inner, heads = w_x.shape[1], dt_bias.shape[1]
    both = conv_w.shape[1]
    f32, bf16 = jnp.float32, jnp.bfloat16
    wide = (inner + width) // chips
    shapes = [((seq, wide), bf16)] * chips + [
        ((seq, loads[0].shape[1]), f32),
        ((seq, both), f32), ((seq, both), f32), ((seq, inner), f32), ((seq, inner), f32),
        ((seq, inner), f32), ((seq, 128), f32), ((heads, seq, seq), f32), ((seq, seq), f32),
        ((seq, both - inner), f32), ((seq, heads), f32), ((seq, heads), f32),
    ]
    return pl.pallas_call(
        lambda *refs: forward_kernel(chips, levels, *refs),
        name="student_forward",
        in_specs=[SMEM] + [pl.BlockSpec(memory_space=pltpu.HBM)] * (INPUTS + LOADS),
        out_specs=[VMEM] * (LOADS + len(shapes)),
        out_shape=[pinned(v.shape, v.dtype) for v in loads]
        + [jax.ShapeDtypeStruct(s, t) for s, t in shapes[:chips]]
        + [pinned(s, t) for s, t in shapes[chips:]],
        scratch_shapes=[
            pltpu.VMEM((seq, width), bf16), pltpu.VMEM((seq, inner), bf16),
            pltpu.VMEM((chips, seq, wide), bf16), *[pltpu.VMEM(v.shape, v.dtype) for v in inputs],
            pltpu.SemaphoreType.DMA((INPUTS + LOADS,)),
        ],
        compiler_params=pltpu.CompilerParams(vmem_limit_bytes=15 << 20),
        cost_estimate=cost(6),
    )(meta, *[pltpu.with_memory_space_constraint(v, pltpu.HBM) for v in (*inputs, *loads)])


def student_backward(d_out, w_out, n_gain, conv_w, a_log, d_skip, saved):
    seq = d_out.shape[0]
    inner, heads = w_out.shape[0], a_log.shape[1]
    both = conv_w.shape[1]
    f32 = jnp.float32
    wide = both // TERM_CHUNKS
    return pl.pallas_call(
        backward_kernel,
        name="student_backward",
        in_specs=[VMEM] * (6 + len(saved)),
        out_specs=VMEM,
        out_shape=jax.ShapeDtypeStruct((seq + TERM_ROWS, wide), jnp.bfloat16),
        scratch_shapes=[
            pltpu.VMEM((8, both), f32), pltpu.VMEM((seq, inner), f32), pltpu.VMEM((seq, inner), f32),
        ],
        compiler_params=pltpu.CompilerParams(vmem_limit_bytes=8 << 20),
        cost_estimate=cost(9),
    )(d_out, *in_vmem([w_out]), n_gain, conv_w, a_log, d_skip, *in_vmem(saved))


def contract_kernel(count, lanes, extra, meta, *refs):
    cols, blocks = refs[:count], refs[count : 2 * count]
    mine, theirs, part = refs[2 * count :]
    f32 = jnp.float32
    seq = cols[0].shape[0]
    part[...] = lax.dot_general(
        jnp.concatenate([c[:, lanes] for c in cols]),
        jnp.concatenate([b[:seq, :] for b in blocks]),
        (((0,), (0,)), ((), ())),
        preferred_element_type=f32,
    ).reshape(part.shape)
    rows = part.shape[0] * part.shape[2]
    width = part.shape[3]
    mine[:rows, :] = part[:, pl.ds(meta[CORE], 1), :, :].reshape(rows, width)
    theirs[:rows, :] = part[:, pl.ds(1 - meta[CORE], 1), :, :].reshape(rows, width).astype(theirs.dtype)
    if extra:
        total = blocks[0][seq:, :].astype(f32)
        for block in blocks[1:]:
            total = total + block[seq:, :].astype(f32)
        mine[rows:, :] = total
        theirs[rows:, :] = total.astype(theirs.dtype)


def contract(meta, cols, lanes, blocks, levels):
    count = len(cols)
    width = blocks[0].shape[1]
    extra = blocks[0].shape[0] - cols[0].shape[0]
    own = (lanes.stop - lanes.start) // (2 * levels)
    rows = levels * own + extra
    return pl.pallas_call(
        lambda *refs: contract_kernel(count, lanes, extra, *refs),
        name="contract",
        in_specs=[SMEM] + [VMEM] * (2 * count),
        out_specs=[VMEM, VMEM],
        out_shape=[
            jax.ShapeDtypeStruct((rows, width), jnp.float32),
            jax.ShapeDtypeStruct((rows, width), jnp.bfloat16),
        ],
        scratch_shapes=[pltpu.VMEM((levels, 2, own, width), jnp.float32)],
        compiler_params=pltpu.CompilerParams(vmem_limit_bytes=6 << 20),
        cost_estimate=cost(0),
    )(meta, *cols, *blocks)


def share_kernel(levels, extra, meta, mine, got, own, *sent):
    rows = (mine.shape[0] - extra) // levels
    for k, to in ((0, own), *((i + 1, m) for i, m in enumerate(sent))):
        at = pl.multiple_of((meta[LEVEL] ^ k) * rows, rows)
        total = mine[pl.ds(at, rows), :] + got[pl.ds(at, rows), :].astype(jnp.float32)
        to[:rows, :] = total.astype(to.dtype)
        if extra:
            tail = slice(mine.shape[0] - extra, mine.shape[0])
            to[rows:, :] = (mine[tail, :] + got[tail, :].astype(jnp.float32)).astype(to.dtype)


def share(meta, mine, got, levels, extra):
    rows = (mine.shape[0] - extra) // levels + extra
    width = mine.shape[1]
    return pl.pallas_call(
        lambda *refs: share_kernel(levels, extra, *refs),
        name="share",
        in_specs=[SMEM, VMEM, VMEM],
        out_specs=[VMEM] * levels,
        out_shape=[jax.ShapeDtypeStruct((rows, width), jnp.float32)]
        + [jax.ShapeDtypeStruct((rows, width), jnp.bfloat16)] * (levels - 1),
        compiler_params=pltpu.CompilerParams(vmem_limit_bytes=3 << 20),
        cost_estimate=cost(0),
    )(meta, mine, got)


def finish_kernel(count, taps, meta, own_a, own_b, *refs):
    got_a, got_b = refs[:count], refs[count : 2 * count]
    g_bcdt, g_conv, g_gain, g_out, terms = refs[2 * count :]
    f32 = jnp.float32
    total = own_a[...]
    for part in got_a:
        total = total + part[...].astype(f32)
    g_out[...] = total
    total = own_b[...]
    for part in got_b:
        total = total + part[...].astype(f32)
    rows, wide = g_bcdt.shape[0], total.shape[1]
    g_bcdt[...] = total[:rows, : g_bcdt.shape[1]]
    terms[...] = total[rows:, :]
    lane = lax.broadcasted_iota(jnp.int32, (1, wide), 1)

    def window(first, width):
        start = meta[DEVICE] * width
        chunk = start // wide
        offset = start - chunk * wide
        left = pltpu.roll(terms[pl.ds(first + chunk, 1), :], wide - offset, 1)
        right = pltpu.roll(terms[pl.ds(first + chunk + 1, 1), :], wide - offset, 1)
        return jnp.where(lane < wide - offset, left, right)[:, :width]

    g_conv[...] = jnp.concatenate(
        [window(k * TERM_CHUNKS, g_conv.shape[1]) for k in range(taps)]
    )
    g_gain[...] = window(taps * TERM_CHUNKS, g_gain.shape[1])


def finish(meta, own_a, own_b, got_a, got_b, shapes):
    f32 = jnp.float32
    return pl.pallas_call(
        lambda *refs: finish_kernel(len(got_a), shapes[1][0], *refs),
        name="finish",
        in_specs=[SMEM] + [VMEM] * (2 + len(got_a) + len(got_b)),
        out_specs=[VMEM] * 4,
        out_shape=[jax.ShapeDtypeStruct(s, f32) for s in shapes],
        scratch_shapes=[pltpu.VMEM((TERM_ROWS, own_b.shape[1]), f32)],
        compiler_params=pltpu.CompilerParams(vmem_limit_bytes=3 << 20),
        cost_estimate=cost(0),
    )(meta, own_a, own_b, *got_a, *got_b)


def swap(values):
    size = lax.axis_size("head")
    return lax.ppermute(values, "head", [(i, i ^ 1) for i in range(size)])


def hop(values, step):
    size = lax.axis_size("head")
    return lax.ppermute(values, "head", [(i, i ^ (2 * step)) for i in range(size)])


def level(values, step):
    size = lax.axis_size("series")
    return lax.ppermute(values, "series", [(i, i ^ step) for i in range(size)])


def teacher_kernel(count, meta, *refs):
    pieces = refs[:count]
    gain, w_gate, w_up, readout, proj, mine, theirs, normed, acc = refs[count:]
    f32 = jnp.float32
    feat = proj.shape[0]
    feat_at = pl.multiple_of(meta[HEAD] * feat, feat)
    strip = 16
    start = 0
    for piece in pieces:
        for at in range(0, piece.shape[0], strip):
            values = piece[at : at + strip, :].astype(f32)
            mean_sq = jnp.mean(values * values, axis=-1, keepdims=True)
            scaled = values * lax.rsqrt(mean_sq + EPS) * gain[...]
            normed[start + at : start + at + strip, :] = scaled.astype(jnp.bfloat16)
        acc[start : start + piece.shape[0], :] = jnp.dot(
            piece[:, pl.ds(feat_at, feat)], proj[...], preferred_element_type=f32
        )
        start += piece.shape[0]
    tile = min(256, w_gate.shape[1])
    for at in range(0, w_gate.shape[1], tile):
        cols = slice(at, at + tile)
        gate = jnp.dot(normed[...], w_gate[:, cols], preferred_element_type=f32)
        upward = jnp.dot(normed[...], w_up[:, cols], preferred_element_type=f32)
        hidden = (gate / (1.0 + jnp.exp(-gate)) * upward).astype(jnp.bfloat16)
        acc[...] += jnp.dot(hidden, readout[cols, :], preferred_element_type=f32)
    rows = mine.shape[0]
    mine[...] = acc[:rows, :]
    theirs[...] = acc[rows:, :].astype(jnp.bfloat16)


def teacher_terms(meta, own, other, teacher_gain, w_gate, w_up, readout, proj):
    pieces = own + other
    rows = sum(p.shape[0] for p in own)
    width, out = w_gate.shape[0], readout.shape[1]
    return pl.pallas_call(
        lambda *refs: teacher_kernel(len(pieces), *refs),
        name="teacher",
        in_specs=[SMEM] + [VMEM] * (len(pieces) + 5),
        out_specs=[VMEM, VMEM],
        out_shape=[
            jax.ShapeDtypeStruct((rows, out), jnp.float32),
            jax.ShapeDtypeStruct((rows, out), jnp.bfloat16),
        ],
        scratch_shapes=[
            pltpu.VMEM((2 * rows, width), jnp.bfloat16),
            pltpu.VMEM((2 * rows, out), jnp.float32),
        ],
        compiler_params=pltpu.CompilerParams(vmem_limit_bytes=(5 << 20) + 2 * rows * (2 * width + 6 * out)),
        cost_estimate=cost(rows / 32),
    )(meta, *pieces, teacher_gain.reshape(1, width), *in_vmem([w_gate, w_up, readout, proj]))


def per_device(
    teacher_in, teacher_gain, w_gate, w_up, readout, distill_proj, building_ids, student_in,
    embed_rows, covariates, cov_proj, student_gain, w_x, w_bcdt, conv_w, dt_bias, a_log, d_skip,
    norm_gain, w_out,
):
    heads, levels = lax.axis_size("head"), lax.axis_size("series")
    chips = heads // 2
    head, z = lax.axis_index("head"), lax.axis_index("series")
    chip, core = head // 2, head % 2
    seq_len = teacher_in.shape[1]
    series_total = teacher_in.shape[0] * heads * levels
    bf16, f32 = jnp.bfloat16, jnp.float32

    own_rows = teacher_in[0]
    across = [hop(own_rows, k) for k in ((1, 2) if chips == 4 else range(1, chips))]
    meta = jnp.stack([head, core, z, chip, z * heads + head]).astype(jnp.int32)
    emb = lax.dynamic_slice_in_dim(embed_rows, building_ids[0], 1, 0)
    cov = lax.dynamic_slice_in_dim(covariates, building_ids[0], 1, 0)
    meta, emb, cov, w_gate = lax.optimization_barrier((meta, emb, cov, w_gate))
    row = [v.reshape(1, -1) for v in (student_gain, dt_bias, a_log, d_skip, norm_gain)]
    fwd = student_forward(
        chips, levels, meta,
        [
            student_in[0], emb, cov, cov_proj, row[0], w_x, w_bcdt.T, conv_w, row[1], row[2], row[3], row[4],
        ],
        [w_out, w_gate, w_up, readout, distill_proj],
    )
    w_out, w_gate, w_up, readout, distill_proj = fwd[:LOADS]
    fwd = fwd[LOADS:]
    cols, output, saved = list(fwd[:chips]), fwd[chips], fwd[chips + 1 :]
    def teach(own):
        return teacher_terms(
            meta, own, [swap(p) for p in own], teacher_gain, w_gate, w_up, readout, distill_proj
        )

    first = teach([own_rows])
    across, first, cols = lax.optimization_barrier((across, first, cols))

    def settle(terms, steps):
        mine, theirs = terms
        both = mine + swap(theirs).astype(f32)
        blocks = [both[i * seq_len : (i + 1) * seq_len] for i in range(len(steps))]
        return [hop(v.astype(bf16), k) if k else v for v, k in zip(blocks, steps)]

    def exchanged():
        return [cols[0]] + [hop(cols[k], k) for k in range(1, chips)]

    if chips == 4:
        half = seq_len // 2
        corner = [hop(across[1][:half], 1), hop(across[0][half:], 2)]
        second = teach(across)
        corner, second, cols = lax.optimization_barrier((corner, second, cols))
        parts = settle(first, (0,)) + settle(second, (1, 2))
        third = teach(corner)
        cols = exchanged()
        third, cols = lax.optimization_barrier((third, cols))
        parts = parts + settle(third, (3,))
    else:
        cols = exchanged()
        parts = settle(first, (0,))
        for k, v in enumerate(across):
            parts = parts + settle(teach([v]), (k + 1,))
    parts, cols = lax.optimization_barrier((parts, cols))
    target = parts[0]
    for part in parts[1:]:
        target = target + part.astype(f32)
    split = w_x.shape[1] // chips

    d_output = ((output - target) / series_total).astype(bf16)
    d_blocks = [d_output] + [hop(d_output, k) for k in range(1, chips)]
    message = student_backward(d_output, w_out, row[4], conv_w, row[2], row[3], saved)
    d_blocks, message = lax.optimization_barrier((d_blocks, message))

    messages = [message] + [hop(message, k) for k in range(1, chips)]
    mine, theirs = contract(meta, cols, slice(0, split), d_blocks, levels)
    own_a, *sent_a = share(meta, mine, swap(theirs), levels, 0)
    got_a = [level(v, k + 1) for k, v in enumerate(sent_a)]
    mine, theirs = contract(meta, cols, slice(split, cols[0].shape[1]), messages, levels)
    own_b, *sent_b = share(meta, mine, swap(theirs), levels, TERM_ROWS)
    got_a, sent_b = lax.optimization_barrier((got_a, sent_b))
    got_b = [level(v, k + 1) for k, v in enumerate(sent_b)]

    devices = heads * levels
    g_bcdt, g_conv, g_gain, g_out = finish(
        meta, own_a, own_b, got_a, got_b,
        [
            (w_bcdt.shape[0] // devices, w_bcdt.shape[1]), (conv_w.shape[0], conv_w.shape[1] // devices),
            (1, norm_gain.shape[0] // devices), (w_out.shape[0] // devices, w_out.shape[1]),
        ],
    )
    return (g_bcdt, g_conv, g_gain.reshape(-1), g_out)


def solution(mesh):
    return jax.shard_map(
        per_device,
        mesh=mesh,
        in_specs=(
            P(("series", "head"), None, None),
            P(),
            P(None, "head"),
            P(None, "head"),
            P("head", None),
            P("head", None),
            P(("series", "head")),
            P(("series", "head"), None, None),
            P(),
            P(),
            P(),
            P(),
            P(),
            P(),
            P(),
            P(),
            P(),
            P(),
            P(),
            P(),
        ),
        out_specs=(
            P(("series", "head"), None),
            P(None, ("series", "head")),
            P(("series", "head")),
            P(("series", "head"), None),
        ),
        check_vma=False,
    )
```

profile of v0, /device:TPU:0, one launch (start us, length us, event | category | flops | bytes accessed | tf_op | source)
XLA Modules:
  0.0 121.8 jit_solution(4419168799989577947)
XLA Ops:
  1.2 2.6 %collective-permute-start = (bf16[128,4096]{1,0:T(8,128)(2,1)}, bf16[128,4096]{1,0:T(8,128)(2,1)}, u32[]{:S(2)}, u32[]{:S(2)}) collective-permute-start(bf16[128,4096]{1,0:T(8,128)(2,1)} %bitcast.20), channel_id=1, source_target_pairs={{0,2},{1,3},{2,0},{3,1},{4,6},{5,7},{6,4},{7,5},{8,10},{9,11},{10,... | collective-permute-start | bytes 3145736 | tf_op jit(solution)/shard_map/ppermute | solution.py:431
  3.7 1.5 %collective-permute-start.1 = (bf16[128,4096]{1,0:T(8,128)(2,1)}, bf16[128,4096]{1,0:T(8,128)(2,1)}, u32[]{:S(2)}, u32[]{:S(2)}) collective-permute-start(bf16[128,4096]{1,0:T(8,128)(2,1)} %bitcast.21), channel_id=1, source_target_pairs={{0,4},{1,5},{2,6},{3,7},{4,0},{5,1},{6,2},{7,3},{8,12},{9,13},{10,... | collective-permute-start | bytes 3145736 | tf_op jit(solution)/shard_map/ppermute | solution.py:431
  6.6 1.2 constant_dynamic-slice_fusion.refs_3_
  7.8 13.3 %student_forward.1 = (bf16[2048,1024]{1,0:T(8,128)(2,1)S(1)}, bf16[4096,1024]{1,0:T(8,128)(2,1)S(1)}, bf16[4096,1024]{1,0:T(8,128)(2,1)S(1)}, bf16[1024,1024]{1,...) custom-call(s32[5]{0:T(128)S(1)} %stack.23.refs_0_, ...), custom_call_target="tpu_custom_call" | custom-call | flops 6000000000 | tf_op jit(solution)/shard_map/student_forward/pallas_call | solution.py:272
  21.1 6.9 %teacher.3 = (f32[128,1024]{1,0:T(8,128)S(1)}, bf16[128,1024]{1,0:T(8,128)(2,1)S(1)}) custom-call(s32[5]{0:T(128)S(1)} %stack.23.refs_0_, bf16[128,4096]{1,0:T(8,128)(2,1)S(1)} %bitcast.22, bf16[128,4096]{1,0:T(8,128)(2,1)S(1)} %collective-permute-done.2.refs_2_, f32[1,4096]{1,0:T(1,128)S(1)} %bitcast.23, ...), custom_call_target="tpu_custom_call" | custom-call | flops 4000000000 | tf_op jit(solution)/shard_map/teacher/pallas_call | solution.py:473
  28.0 1.2 %collective-permute-done.1.refs_2_ = bf16[128,4096]{1,0:T(8,128)(2,1)} collective-permute-done((bf16[128,4096]{1,0:T(8,128)(2,1)}, bf16[128,4096]{1,0:T(8,128)(2,1)}, u32[]{:S(2)}, u32[]{:S(2)}) %collective-permute-start.1) | collective-permute-done | bytes 1048608 | tf_op jit(solution)/shard_map/ppermute | solution.py:431
  32.4 1.7 %collective-permute-start.5 = (bf16[64,4096]{1,0:T(8,128)(2,1)S(1)}, bf16[64,4096]{1,0:T(8,128)(2,1)S(1)}, u32[]{:S(2)}, u32[]{:S(2)}) collective-permute-start(bf16[64,4096]{1,0:T(8,128)(2,1)S(1)} %slice.15), channel_id=1, source_target_pairs={{0,4},{1,5},{2,6},{3,7},{4,0},{5,1},{6,2},{7,3},{8,12},{9,13},{10,... | collective-permute-start | bytes 1572872 | tf_op jit(solution)/shard_map/ppermute | solution.py:431
  34.1 13.4 %teacher.4 = (f32[256,1024]{1,0:T(8,128)S(1)}, bf16[256,1024]{1,0:T(8,128)(2,1)S(1)}) custom-call(s32[5]{0:T(128)S(1)} %stack.23.refs_0_, bf16[128,4096]{1,0:T(8,128)(2,1)} %collective-permute-done.refs_1_, bf16[128,4096]{1,0:T(8,128)(2,1)} %collective-permute-done.1.refs_2_, bf16[128,4096]{1,0:T(8,128)(2,1)S(1)} %collective-permute-done.6.refs_3_, ...), custom_call_target="tpu_custom_call" | custom-call | flops 8000000000 | tf_op jit(solution)/shard_map/teacher/pallas_call | solution.py:473
  48.6 1.5 %collective-permute-start.13 = (bf16[128,768]{1,0:T(8,128)(2,1)S(1)}, bf16[128,768]{1,0:T(8,128)(2,1)S(1)}, u32[]{:S(2)}, u32[]{:S(2)}) collective-permute-start(bf16[128,768]{1,0:T(8,128)(2,1)S(1)} %get-tuple-element.123), channel_id=1, source_target_pairs={{0,2},{1,3},{2,0},{3,1},{4,6},{5,7},{6,4},{7,5},{8,10},{9,11},{10,... | collective-permute-start | bytes 589832 | tf_op jit(solution)/shard_map/ppermute | solution.py:431
  50.6 1.8 %collective-permute-start.15 = (bf16[128,768]{1,0:T(8,128)(2,1)S(1)}, bf16[128,768]{1,0:T(8,128)(2,1)S(1)}, u32[]{:S(2)}, u32[]{:S(2)}) collective-permute-start(bf16[128,768]{1,0:T(8,128)(2,1)S(1)} %get-tuple-element.125), channel_id=1, source_target_pairs={{0,6},{1,7},{2,4},{3,5},{4,2},{5,3},{6,0},{7,1},{8,14},{9,15},{10,... | collective-permute-start | bytes 589832 | tf_op jit(solution)/shard_map/ppermute | solution.py:431
  52.4 7.2 %teacher.5 = (f32[128,1024]{1,0:T(8,128)S(1)}, bf16[128,1024]{1,0:T(8,128)(2,1)S(1)}) custom-call(s32[5]{0:T(128)S(1)} %stack.23.refs_0_, bf16[64,4096]{1,0:T(8,128)(2,1)S(1)} %collective-permute-done.4.refs_1_, bf16[64,4096]{1,0:T(8,128)(2,1)S(1)} %collective-permute-done.5.refs_2_, bf16[64,4096]{1,0:T(8,128)(2,1)S(1)} %collective-permute-done.11.refs_3_, ...), custom_call_target="tpu_custom_call" | custom-call | flops 4000000000 | tf_op jit(solution)/shard_map/teacher/pallas_call | solution.py:473
  59.7 1.2 collective-permute-done.14.refs_3_
  63.2 1.8 %collective-permute-start.17 = (bf16[128,1024]{1,0:T(8,128)(2,1)S(1)}, bf16[128,1024]{1,0:T(8,128)(2,1)S(1)}, u32[]{:S(2)}, u32[]{:S(2)}) collective-permute-start(bf16[128,1024]{1,0:T(8,128)(2,1)S(1)} %add_convert_fusion.1), channel_id=1, source_target_pairs={{0,6},{1,7},{2,4},{3,5},{4,2},{5,3},{6,0},{7,1},{8,14},{9,15},{10,... | collective-permute-start | bytes 786440 | tf_op jit(solution)/shard_map/ppermute | solution.py:431
  65.1 5.0 %collective-permute-done.10 = bf16[128,1024]{1,0:T(8,128)(2,1)S(1)} collective-permute-done((bf16[128,1024]{1,0:T(8,128)(2,1)S(1)}, bf16[128,1024]{1,0:T(8,128)(2,1)S(1)}, u32[]{:S(2)}, u32[]{:S(2)}) %collective-permute-start.10) | collective-permute-done | bytes 262176 | tf_op jit(solution)/shard_map/ppermute | solution.py:431
  70.1 1.3 %collective-permute-done.9 = bf16[128,1024]{1,0:T(8,128)(2,1)S(1)} collective-permute-done((bf16[128,1024]{1,0:T(8,128)(2,1)S(1)}, bf16[128,1024]{1,0:T(8,128)(2,1)S(1)}, u32[]{:S(2)}, u32[]{:S(2)}) %collective-permute-start.9) | collective-permute-done | bytes 262176 | tf_op jit(solution)/shard_map/ppermute | solution.py:431
  71.4 5.5 %collective-permute-done.17 = bf16[128,1024]{1,0:T(8,128)(2,1)S(1)} collective-permute-done((bf16[128,1024]{1,0:T(8,128)(2,1)S(1)}, bf16[128,1024]{1,0:T(8,128)(2,1)S(1)}, u32[]{:S(2)}, u32[]{:S(2)}) %collective-permute-start.17) | collective-permute-done | bytes 262176 | tf_op jit(solution)/shard_map/ppermute | solution.py:431
  77.1 1.3 %collective-permute-start.18 = (bf16[128,1024]{1,0:T(8,128)(2,1)S(1)}, bf16[128,1024]{1,0:T(8,128)(2,1)S(1)}, u32[]{:S(2)}, u32[]{:S(2)}) collective-permute-start(bf16[128,1024]{1,0:T(8,128)(2,1)S(1)} %multiply_convert_fusion.d_out.refs_5_), channel_id=1, source_target_pairs={{0,2},{1,3},{2,0},{3,1},{4,6},{5,7},{6,4},{7,5},{8,10},{9,11},{10,... | collective-permute-start | bytes 786440 | tf_op jit(solution)/shard_map/ppermute | solution.py:431
  78.9 1.8 %collective-permute-start.20 = (bf16[128,1024]{1,0:T(8,128)(2,1)S(1)}, bf16[128,1024]{1,0:T(8,128)(2,1)S(1)}, u32[]{:S(2)}, u32[]{:S(2)}) collective-permute-start(bf16[128,1024]{1,0:T(8,128)(2,1)S(1)} %multiply_convert_fusion.d_out.refs_5_), channel_id=1, source_target_pairs={{0,6},{1,7},{2,4},{3,5},{4,2},{5,3},{6,0},{7,1},{8,14},{9,15},{10,... | collective-permute-start | bytes 786440 | tf_op jit(solution)/shard_map/ppermute | solution.py:431
  80.7 6.7 %student_backward.1.refs_5_ = bf16[160,384]{1,0:T(8,128)(2,1)S(1)} custom-call(bf16[128,1024]{1,0:T(8,128)(2,1)S(1)} %multiply_convert_fusion.d_out.refs_5_, bf16[2048,1024]{1,0:T(8,128)(2,1)S(1)} %get-tuple-element.141.w_out, f32[1,2048]{1,0:T(1,128)S(1)} %bitcast.27, f32[4,2304]{1,0:T(4,128)S(1)} %copy-done.4, f32[1,32]{1,0:T(1,128)S(1)} %bitcast.29, ...), custom_call_target="tpu_custom_call" | custom-call | flops 8999999488 | tf_op jit(solution)/shard_map/student_backward/pallas_call | solution.py:296
  87.4 3.9 %collective-permute-done.19.refs_7_ = bf16[128,1024]{1,0:T(8,128)(2,1)S(1)} collective-permute-done((bf16[128,1024]{1,0:T(8,128)(2,1)S(1)}, bf16[128,1024]{1,0:T(8,128)(2,1)S(1)}, u32[]{:S(2)}, u32[]{:S(2)}) %collective-permute-start.19) | collective-permute-done | bytes 262176 | tf_op jit(solution)/shard_map/ppermute | solution.py:431
  91.4 1.4 %contract.2 = (f32[256,1024]{1,0:T(8,128)S(1)}, bf16[256,1024]{1,0:T(8,128)(2,1)S(1)}) custom-call(s32[5]{0:T(128)S(1)} %stack.23.refs_0_, bf16[128,768]{1,0:T(8,128)(2,1)S(1)} %get-tuple-element.132.refs_1_, bf16[128,768]{1,0:T(8,128)(2,1)S(1)} %collective-permute-done.13.refs_2_, bf16[128,768]{1,0:T(8,128)(2,1)S(1)} %collective-permute-done.14.refs_3_, ...), custom_call_target="tpu_custom_call" | custom-call | tf_op jit(solution)/shard_map/contract/pallas_call | solution.py:339
  94.6 1.8 %collective-permute-start.24 = (bf16[160,384]{1,0:T(8,128)(2,1)S(1)}, bf16[160,384]{1,0:T(8,128)(2,1)S(1)}, u32[]{:S(2)}, u32[]{:S(2)}) collective-permute-start(bf16[160,384]{1,0:T(8,128)(2,1)S(1)} %student_backward.1.refs_5_), channel_id=1, source_target_pairs={{0,6},{1,7},{2,4},{3,5},{4,2},{5,3},{6,0},{7,1},{8,14},{9,15},{10,... | collective-permute-start | bytes 368648 | tf_op jit(solution)/shard_map/ppermute | solution.py:431
  97.0 1.6 %collective-permute-start.26 = (bf16[64,1024]{1,0:T(8,128)(2,1)S(1)}, bf16[64,1024]{1,0:T(8,128)(2,1)S(1)}, u32[]{:S(2)}, u32[]{:S(2)}) collective-permute-start(bf16[64,1024]{1,0:T(8,128)(2,1)S(1)} %get-tuple-element.164), channel_id=1, source_target_pairs={{0,8},{8,0},{16,24},{24,16},{1,9},{9,1},{17,25},{25,17},{2,10},{10... | collective-permute-start | bytes 393224 | tf_op jit(solution)/shard_map/ppermute | solution.py:436
  98.7 2.6 %collective-permute-start.27 = (bf16[64,1024]{1,0:T(8,128)(2,1)S(1)}, bf16[64,1024]{1,0:T(8,128)(2,1)S(1)}, u32[]{:S(2)}, u32[]{:S(2)}) collective-permute-start(bf16[64,1024]{1,0:T(8,128)(2,1)S(1)} %get-tuple-element.165), channel_id=1, source_target_pairs={{0,16},{8,24},{16,0},{24,8},{1,17},{9,25},{17,1},{25,9},{2,18},{10... | collective-permute-start | bytes 393224 | tf_op jit(solution)/shard_map/ppermute | solution.py:436
  101.3 1.4 %collective-permute-start.28 = (bf16[64,1024]{1,0:T(8,128)(2,1)S(1)}, bf16[64,1024]{1,0:T(8,128)(2,1)S(1)}, u32[]{:S(2)}, u32[]{:S(2)}) collective-permute-start(bf16[64,1024]{1,0:T(8,128)(2,1)S(1)} %get-tuple-element.166), channel_id=1, source_target_pairs={{0,24},{8,16},{16,8},{24,0},{1,25},{9,17},{17,9},{25,1},{2,26},{10... | collective-permute-start | bytes 393224 | tf_op jit(solution)/shard_map/ppermute | solution.py:436
  103.6 1.3 %collective-permute-done.25.refs_2_ = bf16[160,384]{1,0:T(8,128)(2,1)S(1)} collective-permute-done((bf16[160,384]{1,0:T(8,128)(2,1)S(1)}, bf16[160,384]{1,0:T(8,128)(2,1)S(1)}, u32[]{:S(2)}, u32[]{:S(2)}) %collective-permute-start.25) | collective-permute-done | bytes 122912 | tf_op jit(solution)/shard_map/ppermute | solution.py:426
  105.5 5.8 %collective-permute-done.27.refs_4_ = bf16[64,1024]{1,0:T(8,128)(2,1)S(1)} collective-permute-done((bf16[64,1024]{1,0:T(8,128)(2,1)S(1)}, bf16[64,1024]{1,0:T(8,128)(2,1)S(1)}, u32[]{:S(2)}, u32[]{:S(2)}) %collective-permute-start.27) | collective-permute-done | bytes 131104 | tf_op jit(solution)/shard_map/ppermute | solution.py:436
  111.4 2.0 %collective-permute-start.29 = (bf16[64,384]{1,0:T(8,128)(2,1)S(1)}, bf16[64,384]{1,0:T(8,128)(2,1)S(1)}, u32[]{:S(2)}, u32[]{:S(2)}) collective-permute-start(bf16[64,384]{1,0:T(8,128)(2,1)S(1)} %get-tuple-element.173), channel_id=1, source_target_pairs={{0,8},{8,0},{16,24},{24,16},{1,9},{9,1},{17,25},{25,17},{2,10},{10... | collective-permute-start | bytes 147464 | tf_op jit(solution)/shard_map/ppermute | solution.py:436
  114.4 1.5 %collective-permute-start.31 = (bf16[64,384]{1,0:T(8,128)(2,1)S(1)}, bf16[64,384]{1,0:T(8,128)(2,1)S(1)}, u32[]{:S(2)}, u32[]{:S(2)}) collective-permute-start(bf16[64,384]{1,0:T(8,128)(2,1)S(1)} %get-tuple-element.175), channel_id=1, source_target_pairs={{0,24},{8,16},{16,8},{24,0},{1,25},{9,17},{17,9},{25,1},{2,26},{10... | collective-permute-start | bytes 147464 | tf_op jit(solution)/shard_map/ppermute | solution.py:436
  116.0 3.1 %collective-permute-done.30.refs_7_ = bf16[64,384]{1,0:T(8,128)(2,1)S(1)} collective-permute-done((bf16[64,384]{1,0:T(8,128)(2,1)S(1)}, bf16[64,384]{1,0:T(8,128)(2,1)S(1)}, u32[]{:S(2)}, u32[]{:S(2)}) %collective-permute-start.30) | collective-permute-done | bytes 49184 | tf_op jit(solution)/shard_map/ppermute | solution.py:436
  119.1 1.3 %collective-permute-done.31.refs_8_ = bf16[64,384]{1,0:T(8,128)(2,1)S(1)} collective-permute-done((bf16[64,384]{1,0:T(8,128)(2,1)S(1)}, bf16[64,384]{1,0:T(8,128)(2,1)S(1)}, u32[]{:S(2)}, u32[]{:S(2)}) %collective-permute-start.31) | collective-permute-done | bytes 49184 | tf_op jit(solution)/shard_map/ppermute | solution.py:436
  120.4 1.4 %finish.1 = (f32[32,288]{1,0:T(8,128)}, f32[4,72]{1,0:T(4,128)}, f32[1,64]{1,0:T(1,128)}, f32[64,1024]{1,0:T(8,128)}) custom-call(s32[5]{0:T(128)S(1)} %stack.23.refs_0_, f32[64,1024]{1,0:T(8,128)S(1)} %get-tuple-element.159.refs_1_, f32[64,384]{1,0:T(8,128)S(1)} %get-tuple-element.163.refs_2_, bf16[64,1024]{1,0:T(8,128)(2,1)S(1)} %collective-permute-done.26.refs_3_, ...), custom_call_target="tpu_custom_call" | custom-call | tf_op jit(solution)/shard_map/finish/pallas_call | solution.py:412
  (68 shorter events, 14.2 us)
Async XLA Ops:
  0.6 20.5 %collective-permute-start.2 = (bf16[128,4096]{1,0:T(8,128)(2,1)}, bf16[128,4096]{1,0:T(8,128)(2,1)S(1)}, u32[]{:S(2)}, u32[]{:S(2)}) collective-permute-start(bf16[128,4096]{1,0:T(8,128)(2,1)} %bitcast.19), channel_id=1, source_target_pairs={{0,1},{1,0},{2,3},{3,2},{4,5},{5,4},{6,7},{7,6},{8,9},{9,8},{10,11... | collective-permute-start | bytes 3145736 | tf_op jit(solution)/shard_map/ppermute | solution.py:426
  1.2 26.9 %collective-permute-start = (bf16[128,4096]{1,0:T(8,128)(2,1)}, bf16[128,4096]{1,0:T(8,128)(2,1)}, u32[]{:S(2)}, u32[]{:S(2)}) collective-permute-start(bf16[128,4096]{1,0:T(8,128)(2,1)} %bitcast.20), channel_id=1, source_target_pairs={{0,2},{1,3},{2,0},{3,1},{4,6},{5,7},{6,4},{7,5},{8,10},{9,11},{10,... | collective-permute-start | bytes 3145736 | tf_op jit(solution)/shard_map/ppermute | solution.py:431
  3.7 25.5 %collective-permute-start.1 = (bf16[128,4096]{1,0:T(8,128)(2,1)}, bf16[128,4096]{1,0:T(8,128)(2,1)}, u32[]{:S(2)}, u32[]{:S(2)}) collective-permute-start(bf16[128,4096]{1,0:T(8,128)(2,1)} %bitcast.21), channel_id=1, source_target_pairs={{0,4},{1,5},{2,6},{3,7},{4,0},{5,1},{6,2},{7,3},{8,12},{9,13},{10,... | collective-permute-start | bytes 3145736 | tf_op jit(solution)/shard_map/ppermute | solution.py:431
  29.3 4.8 %collective-permute-start.6 = (bf16[128,4096]{1,0:T(8,128)(2,1)}, bf16[128,4096]{1,0:T(8,128)(2,1)S(1)}, u32[]{:S(2)}, u32[]{:S(2)}) collective-permute-start(bf16[128,4096]{1,0:T(8,128)(2,1)} %collective-permute-done.refs_1_), channel_id=1, source_target_pairs={{0,1},{1,0},{2,3},{3,2},{4,5},{5,4},{6,7},{7,6},{8,9},{9,8},{10,11... | collective-permute-start | bytes 3145736 | tf_op jit(solution)/shard_map/ppermute | solution.py:426
  29.3 4.8 %collective-permute-start.7 = (bf16[128,4096]{1,0:T(8,128)(2,1)}, bf16[128,4096]{1,0:T(8,128)(2,1)S(1)}, u32[]{:S(2)}, u32[]{:S(2)}) collective-permute-start(bf16[128,4096]{1,0:T(8,128)(2,1)} %collective-permute-done.1.refs_2_), channel_id=1, source_target_pairs={{0,1},{1,0},{2,3},{3,2},{4,5},{5,4},{6,7},{7,6},{8,9},{9,8},{10,11... | collective-permute-start | bytes 3145736 | tf_op jit(solution)/shard_map/ppermute | solution.py:426
  31.9 15.5 %collective-permute-start.4 = (bf16[64,4096]{1,0:T(8,128)(2,1)S(1)}, bf16[64,4096]{1,0:T(8,128)(2,1)S(1)}, u32[]{:S(2)}, u32[]{:S(2)}) collective-permute-start(bf16[64,4096]{1,0:T(8,128)(2,1)S(1)} %slice.14), channel_id=1, source_target_pairs={{0,2},{1,3},{2,0},{3,1},{4,6},{5,7},{6,4},{7,5},{8,10},{9,11},{10,... | collective-permute-start | bytes 1572872 | tf_op jit(solution)/shard_map/ppermute | solution.py:431
  32.4 15.1 %collective-permute-start.5 = (bf16[64,4096]{1,0:T(8,128)(2,1)S(1)}, bf16[64,4096]{1,0:T(8,128)(2,1)S(1)}, u32[]{:S(2)}, u32[]{:S(2)}) collective-permute-start(bf16[64,4096]{1,0:T(8,128)(2,1)S(1)} %slice.15), channel_id=1, source_target_pairs={{0,4},{1,5},{2,6},{3,7},{4,0},{5,1},{6,2},{7,3},{8,12},{9,13},{10,... | collective-permute-start | bytes 1572872 | tf_op jit(solution)/shard_map/ppermute | solution.py:431
  47.5 2.6 %collective-permute-start.11 = (bf16[64,4096]{1,0:T(8,128)(2,1)S(1)}, bf16[64,4096]{1,0:T(8,128)(2,1)S(1)}, u32[]{:S(2)}, u32[]{:S(2)}) collective-permute-start(bf16[64,4096]{1,0:T(8,128)(2,1)S(1)} %collective-permute-done.4.refs_1_), channel_id=1, source_target_pairs={{0,1},{1,0},{2,3},{3,2},{4,5},{5,4},{6,7},{7,6},{8,9},{9,8},{10,11... | collective-permute-start | bytes 1572872 | tf_op jit(solution)/shard_map/ppermute | solution.py:426
  47.6 3.0 %collective-permute-start.12 = (bf16[64,4096]{1,0:T(8,128)(2,1)S(1)}, bf16[64,4096]{1,0:T(8,128)(2,1)S(1)}, u32[]{:S(2)}, u32[]{:S(2)}) collective-permute-start(bf16[64,4096]{1,0:T(8,128)(2,1)S(1)} %collective-permute-done.5.refs_2_), channel_id=1, source_target_pairs={{0,1},{1,0},{2,3},{3,2},{4,5},{5,4},{6,7},{7,6},{8,9},{9,8},{10,11... | collective-permute-start | bytes 1572872 | tf_op jit(solution)/shard_map/ppermute | solution.py:426
  48.1 12.8 %collective-permute-start.8 = (bf16[256,1024]{1,0:T(8,128)(2,1)S(1)}, bf16[256,1024]{1,0:T(8,128)(2,1)S(1)}, u32[]{:S(2)}, u32[]{:S(2)}) collective-permute-start(bf16[256,1024]{1,0:T(8,128)(2,1)S(1)} %get-tuple-element.117), channel_id=1, source_target_pairs={{0,1},{1,0},{2,3},{3,2},{4,5},{5,4},{6,7},{7,6},{8,9},{9,8},{10,11... | collective-permute-start | bytes 1572872 | tf_op jit(solution)/shard_map/ppermute | solution.py:426
  48.2 16.9 %collective-permute-start.3 = (bf16[128,1024]{1,0:T(8,128)(2,1)S(1)}, bf16[128,1024]{1,0:T(8,128)(2,1)S(1)}, u32[]{:S(2)}, u32[]{:S(2)}) collective-permute-start(bf16[128,1024]{1,0:T(8,128)(2,1)S(1)} %get-tuple-element.107), channel_id=1, source_target_pairs={{0,1},{1,0},{2,3},{3,2},{4,5},{5,4},{6,7},{7,6},{8,9},{9,8},{10,11... | collective-permute-start | bytes 786440 | tf_op jit(solution)/shard_map/ppermute | solution.py:426
  48.6 11.1 %collective-permute-start.13 = (bf16[128,768]{1,0:T(8,128)(2,1)S(1)}, bf16[128,768]{1,0:T(8,128)(2,1)S(1)}, u32[]{:S(2)}, u32[]{:S(2)}) collective-permute-start(bf16[128,768]{1,0:T(8,128)(2,1)S(1)} %get-tuple-element.123), channel_id=1, source_target_pairs={{0,2},{1,3},{2,0},{3,1},{4,6},{5,7},{6,4},{7,5},{8,10},{9,11},{10,... | collective-permute-start | bytes 589832 | tf_op jit(solution)/shard_map/ppermute | solution.py:431
  50.1 10.8 %collective-permute-start.14 = (bf16[128,768]{1,0:T(8,128)(2,1)S(1)}, bf16[128,768]{1,0:T(8,128)(2,1)S(1)}, u32[]{:S(2)}, u32[]{:S(2)}) collective-permute-start(bf16[128,768]{1,0:T(8,128)(2,1)S(1)} %get-tuple-element.124), channel_id=1, source_target_pairs={{0,4},{1,5},{2,6},{3,7},{4,0},{5,1},{6,2},{7,3},{8,12},{9,13},{10,... | collective-permute-start | bytes 589832 | tf_op jit(solution)/shard_map/ppermute | solution.py:431
  50.6 10.3 %collective-permute-start.15 = (bf16[128,768]{1,0:T(8,128)(2,1)S(1)}, bf16[128,768]{1,0:T(8,128)(2,1)S(1)}, u32[]{:S(2)}, u32[]{:S(2)}) collective-permute-start(bf16[128,768]{1,0:T(8,128)(2,1)S(1)} %get-tuple-element.125), channel_id=1, source_target_pairs={{0,6},{1,7},{2,4},{3,5},{4,2},{5,3},{6,0},{7,1},{8,14},{9,15},{10,... | collective-permute-start | bytes 589832 | tf_op jit(solution)/shard_map/ppermute | solution.py:431
  60.9 2.2 %collective-permute-start.16 = (bf16[128,1024]{1,0:T(8,128)(2,1)S(1)}, bf16[128,1024]{1,0:T(8,128)(2,1)S(1)}, u32[]{:S(2)}, u32[]{:S(2)}) collective-permute-start(bf16[128,1024]{1,0:T(8,128)(2,1)S(1)} %get-tuple-element.127), channel_id=1, source_target_pairs={{0,1},{1,0},{2,3},{3,2},{4,5},{5,4},{6,7},{7,6},{8,9},{9,8},{10,11... | collective-permute-start | bytes 786440 | tf_op jit(solution)/shard_map/ppermute | solution.py:426
  61.3 8.8 %collective-permute-start.10 = (bf16[128,1024]{1,0:T(8,128)(2,1)S(1)}, bf16[128,1024]{1,0:T(8,128)(2,1)S(1)}, u32[]{:S(2)}, u32[]{:S(2)}) collective-permute-start(bf16[128,1024]{1,0:T(8,128)(2,1)S(1)} %get-tuple-element.180), channel_id=1, source_target_pairs={{0,4},{1,5},{2,6},{3,7},{4,0},{5,1},{6,2},{7,3},{8,12},{9,13},{10,... | collective-permute-start | bytes 786440 | tf_op jit(solution)/shard_map/ppermute | solution.py:431
  62.2 9.1 %collective-permute-start.9 = (bf16[128,1024]{1,0:T(8,128)(2,1)S(1)}, bf16[128,1024]{1,0:T(8,128)(2,1)S(1)}, u32[]{:S(2)}, u32[]{:S(2)}) collective-permute-start(bf16[128,1024]{1,0:T(8,128)(2,1)S(1)} %get-tuple-element.181), channel_id=1, source_target_pairs={{0,2},{1,3},{2,0},{3,1},{4,6},{5,7},{6,4},{7,5},{8,10},{9,11},{10,... | collective-permute-start | bytes 786440 | tf_op jit(solution)/shard_map/ppermute | solution.py:431
  63.2 13.7 %collective-permute-start.17 = (bf16[128,1024]{1,0:T(8,128)(2,1)S(1)}, bf16[128,1024]{1,0:T(8,128)(2,1)S(1)}, u32[]{:S(2)}, u32[]{:S(2)}) collective-permute-start(bf16[128,1024]{1,0:T(8,128)(2,1)S(1)} %add_convert_fusion.1), channel_id=1, source_target_pairs={{0,6},{1,7},{2,4},{3,5},{4,2},{5,3},{6,0},{7,1},{8,14},{9,15},{10,... | collective-permute-start | bytes 786440 | tf_op jit(solution)/shard_map/ppermute | solution.py:431
  77.1 10.3 %collective-permute-start.18 = (bf16[128,1024]{1,0:T(8,128)(2,1)S(1)}, bf16[128,1024]{1,0:T(8,128)(2,1)S(1)}, u32[]{:S(2)}, u32[]{:S(2)}) collective-permute-start(bf16[128,1024]{1,0:T(8,128)(2,1)S(1)} %multiply_convert_fusion.d_out.refs_5_), channel_id=1, source_target_pairs={{0,2},{1,3},{2,0},{3,1},{4,6},{5,7},{6,4},{7,5},{8,10},{9,11},{10,... | collective-permute-start | bytes 786440 | tf_op jit(solution)/shard_map/ppermute | solution.py:431
  78.4 13.0 %collective-permute-start.19 = (bf16[128,1024]{1,0:T(8,128)(2,1)S(1)}, bf16[128,1024]{1,0:T(8,128)(2,1)S(1)}, u32[]{:S(2)}, u32[]{:S(2)}) collective-permute-start(bf16[128,1024]{1,0:T(8,128)(2,1)S(1)} %multiply_convert_fusion.d_out.refs_5_), channel_id=1, source_target_pairs={{0,4},{1,5},{2,6},{3,7},{4,0},{5,1},{6,2},{7,3},{8,12},{9,13},{10,... | collective-permute-start | bytes 786440 | tf_op jit(solution)/shard_map/ppermute | solution.py:431
  78.9 12.4 %collective-permute-start.20 = (bf16[128,1024]{1,0:T(8,128)(2,1)S(1)}, bf16[128,1024]{1,0:T(8,128)(2,1)S(1)}, u32[]{:S(2)}, u32[]{:S(2)}) collective-permute-start(bf16[128,1024]{1,0:T(8,128)(2,1)S(1)} %multiply_convert_fusion.d_out.refs_5_), channel_id=1, source_target_pairs={{0,6},{1,7},{2,4},{3,5},{4,2},{5,3},{6,0},{7,1},{8,14},{9,15},{10,... | collective-permute-start | bytes 786440 | tf_op jit(solution)/shard_map/ppermute | solution.py:431
  92.8 3.6 %collective-permute-start.21 = (bf16[256,1024]{1,0:T(8,128)(2,1)S(1)}, bf16[256,1024]{1,0:T(8,128)(2,1)S(1)}, u32[]{:S(2)}, u32[]{:S(2)}) collective-permute-start(bf16[256,1024]{1,0:T(8,128)(2,1)S(1)} %get-tuple-element.158), channel_id=1, source_target_pairs={{0,1},{1,0},{2,3},{3,2},{4,5},{5,4},{6,7},{7,6},{8,9},{9,8},{10,11... | collective-permute-start | bytes 1572872 | tf_op jit(solution)/shard_map/ppermute | solution.py:426
  92.8 8.4 %collective-permute-start.22 = (bf16[160,384]{1,0:T(8,128)(2,1)S(1)}, bf16[160,384]{1,0:T(8,128)(2,1)S(1)}, u32[]{:S(2)}, u32[]{:S(2)}) collective-permute-start(bf16[160,384]{1,0:T(8,128)(2,1)S(1)} %student_backward.1.refs_5_), channel_id=1, source_target_pairs={{0,2},{1,3},{2,0},{3,1},{4,6},{5,7},{6,4},{7,5},{8,10},{9,11},{10,... | collective-permute-start | bytes 368648 | tf_op jit(solution)/shard_map/ppermute | solution.py:431
  93.7 8.9 %collective-permute-start.23 = (bf16[160,384]{1,0:T(8,128)(2,1)S(1)}, bf16[160,384]{1,0:T(8,128)(2,1)S(1)}, u32[]{:S(2)}, u32[]{:S(2)}) collective-permute-start(bf16[160,384]{1,0:T(8,128)(2,1)S(1)} %student_backward.1.refs_5_), channel_id=1, source_target_pairs={{0,4},{1,5},{2,6},{3,7},{4,0},{5,1},{6,2},{7,3},{8,12},{9,13},{10,... | collective-permute-start | bytes 368648 | tf_op jit(solution)/shard_map/ppermute | solution.py:431
  94.6 8.0 %collective-permute-start.24 = (bf16[160,384]{1,0:T(8,128)(2,1)S(1)}, bf16[160,384]{1,0:T(8,128)(2,1)S(1)}, u32[]{:S(2)}, u32[]{:S(2)}) collective-permute-start(bf16[160,384]{1,0:T(8,128)(2,1)S(1)} %student_backward.1.refs_5_), channel_id=1, source_target_pairs={{0,6},{1,7},{2,4},{3,5},{4,2},{5,3},{6,0},{7,1},{8,14},{9,15},{10,... | collective-permute-start | bytes 368648 | tf_op jit(solution)/shard_map/ppermute | solution.py:431
  97.0 8.5 %collective-permute-start.26 = (bf16[64,1024]{1,0:T(8,128)(2,1)S(1)}, bf16[64,1024]{1,0:T(8,128)(2,1)S(1)}, u32[]{:S(2)}, u32[]{:S(2)}) collective-permute-start(bf16[64,1024]{1,0:T(8,128)(2,1)S(1)} %get-tuple-element.164), channel_id=1, source_target_pairs={{0,8},{8,0},{16,24},{24,16},{1,9},{9,1},{17,25},{25,17},{2,10},{10... | collective-permute-start | bytes 393224 | tf_op jit(solution)/shard_map/ppermute | solution.py:436
  98.7 12.7 %collective-permute-start.27 = (bf16[64,1024]{1,0:T(8,128)(2,1)S(1)}, bf16[64,1024]{1,0:T(8,128)(2,1)S(1)}, u32[]{:S(2)}, u32[]{:S(2)}) collective-permute-start(bf16[64,1024]{1,0:T(8,128)(2,1)S(1)} %get-tuple-element.165), channel_id=1, source_target_pairs={{0,16},{8,24},{16,0},{24,8},{1,17},{9,25},{17,1},{25,9},{2,18},{10... | collective-permute-start | bytes 393224 | tf_op jit(solution)/shard_map/ppermute | solution.py:436
  101.3 10.1 %collective-permute-start.28 = (bf16[64,1024]{1,0:T(8,128)(2,1)S(1)}, bf16[64,1024]{1,0:T(8,128)(2,1)S(1)}, u32[]{:S(2)}, u32[]{:S(2)}) collective-permute-start(bf16[64,1024]{1,0:T(8,128)(2,1)S(1)} %get-tuple-element.166), channel_id=1, source_target_pairs={{0,24},{8,16},{16,8},{24,0},{1,25},{9,17},{17,9},{25,1},{2,26},{10... | collective-permute-start | bytes 393224 | tf_op jit(solution)/shard_map/ppermute | solution.py:436
  103.5 1.4 %collective-permute-start.25 = (bf16[160,384]{1,0:T(8,128)(2,1)S(1)}, bf16[160,384]{1,0:T(8,128)(2,1)S(1)}, u32[]{:S(2)}, u32[]{:S(2)}) collective-permute-start(bf16[160,384]{1,0:T(8,128)(2,1)S(1)} %get-tuple-element.162), channel_id=1, source_target_pairs={{0,1},{1,0},{2,3},{3,2},{4,5},{5,4},{6,7},{7,6},{8,9},{9,8},{10,11... | collective-permute-start | bytes 368648 | tf_op jit(solution)/shard_map/ppermute | solution.py:426
  111.4 4.6 %collective-permute-start.29 = (bf16[64,384]{1,0:T(8,128)(2,1)S(1)}, bf16[64,384]{1,0:T(8,128)(2,1)S(1)}, u32[]{:S(2)}, u32[]{:S(2)}) collective-permute-start(bf16[64,384]{1,0:T(8,128)(2,1)S(1)} %get-tuple-element.173), channel_id=1, source_target_pairs={{0,8},{8,0},{16,24},{24,16},{1,9},{9,1},{17,25},{25,17},{2,10},{10... | collective-permute-start | bytes 147464 | tf_op jit(solution)/shard_map/ppermute | solution.py:436
  113.3 5.7 %collective-permute-start.30 = (bf16[64,384]{1,0:T(8,128)(2,1)S(1)}, bf16[64,384]{1,0:T(8,128)(2,1)S(1)}, u32[]{:S(2)}, u32[]{:S(2)}) collective-permute-start(bf16[64,384]{1,0:T(8,128)(2,1)S(1)} %get-tuple-element.174), channel_id=1, source_target_pairs={{0,16},{8,24},{16,0},{24,8},{1,17},{9,25},{17,1},{25,9},{2,18},{10... | collective-permute-start | bytes 147464 | tf_op jit(solution)/shard_map/ppermute | solution.py:436
  114.4 6.0 %collective-permute-start.31 = (bf16[64,384]{1,0:T(8,128)(2,1)S(1)}, bf16[64,384]{1,0:T(8,128)(2,1)S(1)}, u32[]{:S(2)}, u32[]{:S(2)}) collective-permute-start(bf16[64,384]{1,0:T(8,128)(2,1)S(1)} %get-tuple-element.175), channel_id=1, source_target_pairs={{0,24},{8,16},{16,8},{24,0},{1,25},{9,17},{17,9},{25,1},{2,26},{10... | collective-permute-start | bytes 147464 | tf_op jit(solution)/shard_map/ppermute | solution.py:436
  (8 other events, 157.0 us)
where the time goes:
time: 122 us
  Pallas kernels  52.4 us (43%)
  starting transfers between devices  33 us (27%)
  waiting for transfers between devices  29.9 us (25%)
  local copies, waits for them, and re-layouts  4.34 us (4%)
  between operations  1.58 us (1%)
    pallas_call x3, Pallas kernels, teacher_terms(): pl.pallas_call(lambda *refs: teacher_kernel(len(pieces), *refs), name='te...  27.5 us
    ppermute x16, starting transfers between devices, hop(): lax.ppermute(values, 'head', [(i, i ^ 2 * step) for i in range(size)])  20.8 us
    ppermute x16, waiting for transfers between devices, hop(): lax.ppermute(values, 'head', [(i, i ^ 2 * step) for i in range(size)])  18.2 us
    pallas_call x1, Pallas kernels, student_forward(): pl.pallas_call(lambda *refs: forward_kernel(chips, levels, *refs), name='...  13.3 us
    ppermute x6, waiting for transfers between devices, level(): return lax.ppermute(values, 'series', [(i, i ^ step) for i in range(size)])  10.4 us
    ppermute x6, starting transfers between devices, level(): return lax.ppermute(values, 'series', [(i, i ^ step) for i in range(size)])  10 us
    pallas_call x1, Pallas kernels, student_backward(): pl.pallas_call(backward_kernel, name='student_backward', in_specs=[VMEM]...  6.73 us
  transfers between devices with their start and end apart: 32, of which 11 were waited for; matrix products, arithmetic and copies ran while one was open for 4% of the time, Pallas kernels for 41%

commit v1 on v0

--- a/solution.py
+++ b/solution.py
@@ -14,6 +14,7 @@
 TERM_ROWS = 32
 TERM_CHUNKS = 6
 LOADS, INPUTS = 5, 12
+NO_COST = pl.CostEstimate(flops=0, transcendentals=0, bytes_accessed=0)
 HEAD, CORE, LEVEL, CHIP, DEVICE = range(5)
 
 
@@ -244,10 +245,6 @@
     message[seq:, :] = jnp.concatenate(packed).astype(bf16)
 
 
-def cost(micros):
-    return pl.CostEstimate(flops=int(micros * 1e9), transcendentals=0, bytes_accessed=0)
-
-
 def pinned(shape, dtype):
     return pltpu.VMEM(shape, dtype)
 
@@ -283,7 +280,7 @@
             pltpu.SemaphoreType.DMA((INPUTS + LOADS,)),
         ],
         compiler_params=pltpu.CompilerParams(vmem_limit_bytes=15 << 20),
-        cost_estimate=cost(6),
+        cost_estimate=NO_COST,
     )(meta, *[pltpu.with_memory_space_constraint(v, pltpu.HBM) for v in (*inputs, *loads)])
 
 
@@ -303,7 +300,7 @@
             pltpu.VMEM((8, both), f32), pltpu.VMEM((seq, inner), f32), pltpu.VMEM((seq, inner), f32),
         ],
         compiler_params=pltpu.CompilerParams(vmem_limit_bytes=8 << 20),
-        cost_estimate=cost(9),
+        cost_estimate=NO_COST,
     )(d_out, *in_vmem([w_out]), n_gain, conv_w, a_log, d_skip, *in_vmem(saved))
 
 
@@ -347,47 +344,68 @@
         ],
         scratch_shapes=[pltpu.VMEM((levels, 2, own, width), jnp.float32)],
         compiler_params=pltpu.CompilerParams(vmem_limit_bytes=6 << 20),
-        cost_estimate=cost(0),
+        cost_estimate=NO_COST,
     )(meta, *cols, *blocks)
 
 
-def share_kernel(levels, extra, meta, mine, got, own, *sent):
-    rows = (mine.shape[0] - extra) // levels
-    for k, to in ((0, own), *((i + 1, m) for i, m in enumerate(sent))):
-        at = pl.multiple_of((meta[LEVEL] ^ k) * rows, rows)
-        total = mine[pl.ds(at, rows), :] + got[pl.ds(at, rows), :].astype(jnp.float32)
-        to[:rows, :] = total.astype(to.dtype)
-        if extra:
-            tail = slice(mine.shape[0] - extra, mine.shape[0])
-            to[rows:, :] = (mine[tail, :] + got[tail, :].astype(jnp.float32)).astype(to.dtype)
-
-
-def share(meta, mine, got, levels, extra):
-    rows = (mine.shape[0] - extra) // levels + extra
-    width = mine.shape[1]
+def share_kernel(levels, extra, meta, mine_a, got_a, mine_b, got_b, own_a, own_b, *sent):
+    f32 = jnp.float32
+
+    def chip_sum(mine, got, at, rows):
+        return mine[pl.ds(at, rows), :] + got[pl.ds(at, rows), :].astype(f32)
+
+    rows_a = mine_a.shape[0] // levels
+    rows_b = (mine_b.shape[0] - extra) // levels
+    width = mine_a.shape[1]
+    tail = chip_sum(mine_b, got_b, levels * rows_b, extra)
+    for k in range(levels):
+        level_at = meta[LEVEL] ^ k
+        part_a = chip_sum(mine_a, got_a, pl.multiple_of(level_at * rows_a, rows_a), rows_a)
+        part_b = chip_sum(mine_b, got_b, pl.multiple_of(level_at * rows_b, rows_b), rows_b)
+        if k == 0:
+            own_a[...] = part_a
+            own_b[:rows_b, :] = part_b
+            own_b[rows_b:, :] = tail
+        else:
+            to = sent[k - 1]
+            if rows_a != rows_b + extra:
+                to[...] = jnp.zeros_like(to)
+            to[:rows_a, :width] = part_a.astype(to.dtype)
+            to[:rows_b, width:] = part_b.astype(to.dtype)
+            to[rows_b : rows_b + extra, width:] = tail.astype(to.dtype)
+
+
+def share(meta, a, b, levels, extra):
+    rows_a = a[0].shape[0] // levels
+    rows_b = (b[0].shape[0] - extra) // levels + extra
+    width_a, width_b = a[0].shape[1], b[0].shape[1]
+    f32 = jnp.float32
     return pl.pallas_call(
         lambda *refs: share_kernel(levels, extra, *refs),
         name="share",
-        in_specs=[SMEM, VMEM, VMEM],
-        out_specs=[VMEM] * levels,
-        out_shape=[jax.ShapeDtypeStruct((rows, width), jnp.float32)]
-        + [jax.ShapeDtypeStruct((rows, width), jnp.bfloat16)] * (levels - 1),
-        compiler_params=pltpu.CompilerParams(vmem_limit_bytes=3 << 20),
-        cost_estimate=cost(0),
-    )(meta, mine, got)
+        in_specs=[SMEM] + [VMEM] * 4,
+        out_specs=[VMEM] * (levels + 1),
+        out_shape=[
+            jax.ShapeDtypeStruct((rows_a, width_a), f32), jax.ShapeDtypeStruct((rows_b, width_b), f32),
+        ]
+        + [jax.ShapeDtypeStruct((max(rows_a, rows_b), width_a + width_b), jnp.bfloat16)] * (levels - 1),
+        compiler_params=pltpu.CompilerParams(vmem_limit_bytes=4 << 20),
+        cost_estimate=NO_COST,
+    )(meta, *a, *b)
 
 
 def finish_kernel(count, taps, meta, own_a, own_b, *refs):
-    got_a, got_b = refs[:count], refs[count : 2 * count]
-    g_bcdt, g_conv, g_gain, g_out, terms = refs[2 * count :]
+    got = refs[:count]
+    g_bcdt, g_conv, g_gain, g_out, terms = refs[count:]
     f32 = jnp.float32
     total = own_a[...]
-    for part in got_a:
-        total = total + part[...].astype(f32)
+    rows, width = own_a.shape
+    for part in got:
+        total = total + part[:rows, :width].astype(f32)
     g_out[...] = total
     total = own_b[...]
-    for part in got_b:
-        total = total + part[...].astype(f32)
+    for part in got:
+        total = total + part[: own_b.shape[0], width:].astype(f32)
     rows, wide = g_bcdt.shape[0], total.shape[1]
     g_bcdt[...] = total[:rows, : g_bcdt.shape[1]]
     terms[...] = total[rows:, :]
@@ -407,18 +425,18 @@
     g_gain[...] = window(taps * TERM_CHUNKS, g_gain.shape[1])
 
 
-def finish(meta, own_a, own_b, got_a, got_b, shapes):
+def finish(meta, own_a, own_b, got, shapes):
     f32 = jnp.float32
     return pl.pallas_call(
-        lambda *refs: finish_kernel(len(got_a), shapes[1][0], *refs),
+        lambda *refs: finish_kernel(len(got), shapes[1][0], *refs),
         name="finish",
-        in_specs=[SMEM] + [VMEM] * (2 + len(got_a) + len(got_b)),
+        in_specs=[SMEM] + [VMEM] * (2 + len(got)),
         out_specs=[VMEM] * 4,
         out_shape=[jax.ShapeDtypeStruct(s, f32) for s in shapes],
         scratch_shapes=[pltpu.VMEM((TERM_ROWS, own_b.shape[1]), f32)],
         compiler_params=pltpu.CompilerParams(vmem_limit_bytes=3 << 20),
-        cost_estimate=cost(0),
-    )(meta, own_a, own_b, *got_a, *got_b)
+        cost_estimate=NO_COST,
+    )(meta, own_a, own_b, *got)
 
 
 def swap(values):
@@ -484,7 +502,7 @@
             pltpu.VMEM((2 * rows, out), jnp.float32),
         ],
         compiler_params=pltpu.CompilerParams(vmem_limit_bytes=(5 << 20) + 2 * rows * (2 * width + 6 * out)),
-        cost_estimate=cost(rows / 32),
+        cost_estimate=NO_COST,
     )(meta, *pieces, teacher_gain.reshape(1, width), *in_vmem([w_gate, w_up, readout, proj]))
 
 
@@ -550,7 +568,6 @@
         parts = settle(first, (0,))
         for k, v in enumerate(across):
             parts = parts + settle(teach([v]), (k + 1,))
-    parts, cols = lax.optimization_barrier((parts, cols))
     target = parts[0]
     for part in parts[1:]:
         target = target + part.astype(f32)
@@ -559,20 +576,19 @@
     d_output = ((output - target) / series_total).astype(bf16)
     d_blocks = [d_output] + [hop(d_output, k) for k in range(1, chips)]
     message = student_backward(d_output, w_out, row[4], conv_w, row[2], row[3], saved)
-    d_blocks, message = lax.optimization_barrier((d_blocks, message))
-
+    message, d_blocks[1], cols = lax.optimization_barrier((message, d_blocks[1], cols))
     messages = [message] + [hop(message, k) for k in range(1, chips)]
-    mine, theirs = contract(meta, cols, slice(0, split), d_blocks, levels)
-    own_a, *sent_a = share(meta, mine, swap(theirs), levels, 0)
-    got_a = [level(v, k + 1) for k, v in enumerate(sent_a)]
-    mine, theirs = contract(meta, cols, slice(split, cols[0].shape[1]), messages, levels)
-    own_b, *sent_b = share(meta, mine, swap(theirs), levels, TERM_ROWS)
-    got_a, sent_b = lax.optimization_barrier((got_a, sent_b))
-    got_b = [level(v, k + 1) for k, v in enumerate(sent_b)]
+    first_a, other_a = contract(meta, cols, slice(0, split), d_blocks, levels)
+    messages, first_a, other_a = lax.optimization_barrier((messages, first_a, other_a))
+    first_b, other_b = contract(meta, cols, slice(split, cols[0].shape[1]), messages, levels)
+    own_a, own_b, *sent = share(
+        meta, (first_a, swap(other_a)), (first_b, swap(other_b)), levels, TERM_ROWS
+    )
+    got = [level(v, k + 1) for k, v in enumerate(sent)]
 
     devices = heads * levels
     g_bcdt, g_conv, g_gain, g_out = finish(
-        meta, own_a, own_b, got_a, got_b,
+        meta, own_a, own_b, got,
         [
             (w_bcdt.shape[0] // devices, w_bcdt.shape[1]), (conv_w.shape[0], conv_w.shape[1] // devices),
             (1, norm_gain.shape[0] // devices), (w_out.shape[0] // devices, w_out.shape[1]),

time: 122 us -> 118 us (0.967)
  starting transfers between devices: 33 us -> 27.2 us
  waiting for transfers between devices: 29.9 us -> 32.7 us
    ppermute x6 -> x3, starting transfers between devices: 10 us -> 4.47 us  [level(): return lax.ppermute(values, 'series', [(i, i ^ step) for i in range(size)])]
    ppermute x6 -> x3, waiting for transfers between devices: 10.4 us -> 13.3 us  [level(): return lax.ppermute(values, 'series', [(i, i ^ step) for i in range(size)])]
  transfers between devices with their start and end apart: 32 -> 29, of which waited for: 11 -> 13; matrix products, arithmetic and copies ran while one was open for 4% -> 3% of each run, Pallas kernels for 41% -> 43%
where the time goes in v1:
time: 118 us; the launch traced here: 117 us
  Pallas kernels  52.3 us (44%)
  waiting for transfers between devices  32.7 us (28%)
  starting transfers between devices  27.2 us (23%)
  local copies, waits for them, and re-layouts  3.3 us (3%)
  between operations  1.54 us (1%)
    pallas_call x3, Pallas kernels, teacher_terms(): pl.pallas_call(lambda *refs: teacher_kernel(len(pieces), *refs), name='te...  27.9 us
    ppermute x16, starting transfers between devices, hop(): lax.ppermute(values, 'head', [(i, i ^ 2 * step) for i in range(size)])  20.4 us
    ppermute x16, waiting for transfers between devices, hop(): lax.ppermute(values, 'head', [(i, i ^ 2 * step) for i in range(size)])  17.8 us
    pallas_call x1, Pallas kernels, student_forward(): pl.pallas_call(lambda *refs: forward_kernel(chips, levels, *refs), name='...  13.3 us
    ppermute x3, waiting for transfers between devices, level(): return lax.ppermute(values, 'series', [(i, i ^ step) for i in range(size)])  13.3 us
    pallas_call x1, Pallas kernels, student_backward(): pl.pallas_call(backward_kernel, name='student_backward', in_specs=[VMEM]...  6.71 us
    ppermute x3, starting transfers between devices, level(): return lax.ppermute(values, 'series', [(i, i ^ step) for i in range(size)])  4.47 us
  transfers between devices with their start and end apart: 29, of which 13 were waited for; matrix products, arithmetic and copies ran while one was open for 3% of the time, Pallas kernels for 43%

profile of v1, /device:TPU:0, one launch (start us, length us, event | category | flops | bytes accessed | tf_op | source)
XLA Modules:
  0.0 117.4 jit_solution(11948926066860332097)
XLA Ops:
  1.2 2.6 %collective-permute-start = (bf16[128,4096]{1,0:T(8,128)(2,1)}, bf16[128,4096]{1,0:T(8,128)(2,1)S(1)}, u32[]{:S(2)}, u32[]{:S(2)}) collective-permute-start(bf16[128,4096]{1,0:T(8,128)(2,1)} %bitcast.20), channel_id=1, source_target_pairs={{0,2},{1,3},{2,0},{3,1},{4,6},{5,7},{6,4},{7,5},{8,10},{9,11},{10,... | collective-permute-start | bytes 3145736 | tf_op jit(solution)/shard_map/ppermute | solution.py:449
  3.7 1.5 %collective-permute-start.1 = (bf16[128,4096]{1,0:T(8,128)(2,1)}, bf16[128,4096]{1,0:T(8,128)(2,1)}, u32[]{:S(2)}, u32[]{:S(2)}) collective-permute-start(bf16[128,4096]{1,0:T(8,128)(2,1)} %bitcast.21), channel_id=1, source_target_pairs={{0,4},{1,5},{2,6},{3,7},{4,0},{5,1},{6,2},{7,3},{8,12},{9,13},{10,... | collective-permute-start | bytes 3145736 | tf_op jit(solution)/shard_map/ppermute | solution.py:449
  6.0 1.2 %constant_dynamic-slice_fusion.refs_3_ = bf16[1,128]{1,0:T(2,128)(2,1)} fusion(bf16[1024,128]{1,0:T(8,128)(2,1)} %param.29, s32[]{:T(128)S(6)} %select_n.17), kind=kLoop, calls=%fused_computation.3 | loop fusion | bytes 516 | tf_op jit(solution)/shard_map/dynamic_slice | solution.py:526
  7.8 13.3 %student_forward.1 = (bf16[2048,1024]{1,0:T(8,128)(2,1)S(1)}, bf16[4096,1024]{1,0:T(8,128)(2,1)S(1)}, bf16[4096,1024]{1,0:T(8,128)(2,1)S(1)}, bf16[1024,1024]{1,...) custom-call(s32[5]{0:T(128)S(1)} %stack.23.refs_0_, ...), custom_call_target="tpu_custom_call" | custom-call | tf_op jit(solution)/shard_map/student_forward/pallas_call | solution.py:269
  21.1 7.6 %teacher.3 = (f32[128,1024]{1,0:T(8,128)S(1)}, bf16[128,1024]{1,0:T(8,128)(2,1)S(1)}) custom-call(s32[5]{0:T(128)S(1)} %stack.23.refs_0_, bf16[128,4096]{1,0:T(8,128)(2,1)S(1)} %bitcast.22, bf16[128,4096]{1,0:T(8,128)(2,1)} %collective-permute-done.2.refs_2_, f32[1,4096]{1,0:T(1,128)S(1)} %bitcast.23, ...), custom_call_target="tpu_custom_call" | custom-call | tf_op jit(solution)/shard_map/teacher/pallas_call | solution.py:491
  29.8 1.1 slice.14
  31.3 1.7 %collective-permute-start.5 = (bf16[64,4096]{1,0:T(8,128)(2,1)S(1)}, bf16[64,4096]{1,0:T(8,128)(2,1)S(1)}, u32[]{:S(2)}, u32[]{:S(2)}) collective-permute-start(bf16[64,4096]{1,0:T(8,128)(2,1)S(1)} %slice.15), channel_id=1, source_target_pairs={{0,4},{1,5},{2,6},{3,7},{4,0},{5,1},{6,2},{7,3},{8,12},{9,13},{10,... | collective-permute-start | bytes 1572872 | tf_op jit(solution)/shard_map/ppermute | solution.py:449
  33.6 13.1 %teacher.4 = (f32[256,1024]{1,0:T(8,128)S(1)}, bf16[256,1024]{1,0:T(8,128)(2,1)S(1)}) custom-call(s32[5]{0:T(128)S(1)} %stack.23.refs_0_, bf16[128,4096]{1,0:T(8,128)(2,1)S(1)} %collective-permute-done.refs_1_, bf16[128,4096]{1,0:T(8,128)(2,1)} %collective-permute-done.1.refs_2_, bf16[128,4096]{1,0:T(8,128)(2,1)S(1)} %collective-permute-done.6.refs_3_, ...), custom_call_target="tpu_custom_call" | custom-call | tf_op jit(solution)/shard_map/teacher/pallas_call | solution.py:491
  48.3 1.3 %collective-permute-start.14 = (bf16[128,768]{1,0:T(8,128)(2,1)S(1)}, bf16[128,768]{1,0:T(8,128)(2,1)S(1)}, u32[]{:S(2)}, u32[]{:S(2)}) collective-permute-start(bf16[128,768]{1,0:T(8,128)(2,1)S(1)} %get-tuple-element.115), channel_id=1, source_target_pairs={{0,4},{1,5},{2,6},{3,7},{4,0},{5,1},{6,2},{7,3},{8,12},{9,13},{10,... | collective-permute-start | bytes 589832 | tf_op jit(solution)/shard_map/ppermute | solution.py:449
  49.6 1.4 %collective-permute-start.15 = (bf16[128,768]{1,0:T(8,128)(2,1)S(1)}, bf16[128,768]{1,0:T(8,128)(2,1)S(1)}, u32[]{:S(2)}, u32[]{:S(2)}) collective-permute-start(bf16[128,768]{1,0:T(8,128)(2,1)S(1)} %get-tuple-element.116), channel_id=1, source_target_pairs={{0,6},{1,7},{2,4},{3,5},{4,2},{5,3},{6,0},{7,1},{8,14},{9,15},{10,... | collective-permute-start | bytes 589832 | tf_op jit(solution)/shard_map/ppermute | solution.py:449
  51.0 7.2 %teacher.5 = (f32[128,1024]{1,0:T(8,128)S(1)}, bf16[128,1024]{1,0:T(8,128)(2,1)S(1)}) custom-call(s32[5]{0:T(128)S(1)} %stack.23.refs_0_, bf16[64,4096]{1,0:T(8,128)(2,1)S(1)} %collective-permute-done.4.refs_1_, bf16[64,4096]{1,0:T(8,128)(2,1)S(1)} %collective-permute-done.5.refs_2_, bf16[64,4096]{1,0:T(8,128)(2,1)S(1)} %collective-permute-done.11.refs_3_, ...), custom_call_target="tpu_custom_call" | custom-call | tf_op jit(solution)/shard_map/teacher/pallas_call | solution.py:491
  58.3 1.5 %collective-permute-done.15.refs_4_ = bf16[128,768]{1,0:T(8,128)(2,1)S(1)} collective-permute-done((bf16[128,768]{1,0:T(8,128)(2,1)S(1)}, bf16[128,768]{1,0:T(8,128)(2,1)S(1)}, u32[]{:S(2)}, u32[]{:S(2)}) %collective-permute-start.15) | collective-permute-done | bytes 196640 | tf_op jit(solution)/shard_map/ppermute | solution.py:449
  61.2 1.5 %collective-permute-start.9 = (bf16[128,1024]{1,0:T(8,128)(2,1)S(1)}, bf16[128,1024]{1,0:T(8,128)(2,1)S(1)}, u32[]{:S(2)}, u32[]{:S(2)}) collective-permute-start(bf16[128,1024]{1,0:T(8,128)(2,1)S(1)} %get-tuple-element.160), channel_id=1, source_target_pairs={{0,2},{1,3},{2,0},{3,1},{4,6},{5,7},{6,4},{7,5},{8,10},{9,11},{10,... | collective-permute-start | bytes 786440 | tf_op jit(solution)/shard_map/ppermute | solution.py:449
  62.7 1.2 %collective-permute-start.17 = (bf16[128,1024]{1,0:T(8,128)(2,1)S(1)}, bf16[128,1024]{1,0:T(8,128)(2,1)S(1)}, u32[]{:S(2)}, u32[]{:S(2)}) collective-permute-start(bf16[128,1024]{1,0:T(8,128)(2,1)S(1)} %add_convert_fusion.1), channel_id=1, source_target_pairs={{0,6},{1,7},{2,4},{3,5},{4,2},{5,3},{6,0},{7,1},{8,14},{9,15},{10,... | collective-permute-start | bytes 786440 | tf_op jit(solution)/shard_map/ppermute | solution.py:449
  64.0 5.1 %collective-permute-done.10 = bf16[128,1024]{1,0:T(8,128)(2,1)S(1)} collective-permute-done((bf16[128,1024]{1,0:T(8,128)(2,1)S(1)}, bf16[128,1024]{1,0:T(8,128)(2,1)S(1)}, u32[]{:S(2)}, u32[]{:S(2)}) %collective-permute-start.10) | collective-permute-done | bytes 262176 | tf_op jit(solution)/shard_map/ppermute | solution.py:449
  69.1 1.2 %collective-permute-done.9 = bf16[128,1024]{1,0:T(8,128)(2,1)S(1)} collective-permute-done((bf16[128,1024]{1,0:T(8,128)(2,1)S(1)}, bf16[128,1024]{1,0:T(8,128)(2,1)S(1)}, u32[]{:S(2)}, u32[]{:S(2)}) %collective-permute-start.9) | collective-permute-done | bytes 262176 | tf_op jit(solution)/shard_map/ppermute | solution.py:449
  70.3 5.6 %collective-permute-done.17 = bf16[128,1024]{1,0:T(8,128)(2,1)S(1)} collective-permute-done((bf16[128,1024]{1,0:T(8,128)(2,1)S(1)}, bf16[128,1024]{1,0:T(8,128)(2,1)S(1)}, u32[]{:S(2)}, u32[]{:S(2)}) %collective-permute-start.17) | collective-permute-done | bytes 262176 | tf_op jit(solution)/shard_map/ppermute | solution.py:449
  77.0 1.5 %collective-permute-start.22 = (bf16[128,1024]{1,0:T(8,128)(2,1)S(1)}, bf16[128,1024]{1,0:T(8,128)(2,1)S(1)}, u32[]{:S(2)}, u32[]{:S(2)}) collective-permute-start(bf16[128,1024]{1,0:T(8,128)(2,1)S(1)} %multiply_convert_fusion.d_out.refs_5_), channel_id=1, source_target_pairs={{0,4},{1,5},{2,6},{3,7},{4,0},{5,1},{6,2},{7,3},{8,12},{9,13},{10,... | collective-permute-start | bytes 786440 | tf_op jit(solution)/shard_map/ppermute | solution.py:449
  78.5 1.2 collective-permute-start.23
  79.7 6.7 %student_backward.1.refs_5_ = bf16[160,384]{1,0:T(8,128)(2,1)S(1)} custom-call(bf16[128,1024]{1,0:T(8,128)(2,1)S(1)} %multiply_convert_fusion.d_out.refs_5_, bf16[2048,1024]{1,0:T(8,128)(2,1)S(1)} %get-tuple-element.119.w_out, f32[1,2048]{1,0:T(1,128)S(1)} %bitcast.27, f32[4,2304]{1,0:T(4,128)S(1)} %copy-done.3, f32[1,32]{1,0:T(1,128)S(1)} %bitcast.29, ...), custom_call_target="tpu_custom_call" | custom-call | tf_op jit(solution)/shard_map/student_backward/pallas_call | solution.py:293
  87.3 1.5 %collective-permute-start.20 = (bf16[160,384]{1,0:T(8,128)(2,1)S(1)}, bf16[160,384]{1,0:T(8,128)(2,1)S(1)}, u32[]{:S(2)}, u32[]{:S(2)}) collective-permute-start(bf16[160,384]{1,0:T(8,128)(2,1)S(1)} %student_backward.1.refs_5_), channel_id=1, source_target_pairs={{0,4},{1,5},{2,6},{3,7},{4,0},{5,1},{6,2},{7,3},{8,12},{9,13},{10,... | collective-permute-start | bytes 368648 | tf_op jit(solution)/shard_map/ppermute | solution.py:449
  88.8 1.2 %collective-permute-start.21 = (bf16[160,384]{1,0:T(8,128)(2,1)S(1)}, bf16[160,384]{1,0:T(8,128)(2,1)S(1)}, u32[]{:S(2)}, u32[]{:S(2)}) collective-permute-start(bf16[160,384]{1,0:T(8,128)(2,1)S(1)} %student_backward.1.refs_5_), channel_id=1, source_target_pairs={{0,6},{1,7},{2,4},{3,5},{4,2},{5,3},{6,0},{7,1},{8,14},{9,15},{10,... | collective-permute-start | bytes 368648 | tf_op jit(solution)/shard_map/ppermute | solution.py:449
  90.0 1.4 %collective-permute-done.23.refs_8_ = bf16[128,1024]{1,0:T(8,128)(2,1)S(1)} collective-permute-done((bf16[128,1024]{1,0:T(8,128)(2,1)S(1)}, bf16[128,1024]{1,0:T(8,128)(2,1)S(1)}, u32[]{:S(2)}, u32[]{:S(2)}) %collective-permute-start.23) | collective-permute-done | bytes 262176 | tf_op jit(solution)/shard_map/ppermute | solution.py:449
  91.4 1.4 %contract.2 = (f32[256,1024]{1,0:T(8,128)S(1)}, bf16[256,1024]{1,0:T(8,128)(2,1)S(1)}) custom-call(s32[5]{0:T(128)S(1)} %stack.23.refs_0_, bf16[128,768]{1,0:T(8,128)(2,1)S(1)} %get-tuple-element.136.refs_1_, bf16[128,768]{1,0:T(8,128)(2,1)S(1)} %collective-permute-done.13.refs_2_, bf16[128,768]{1,0:T(8,128)(2,1)S(1)} %collective-permute-done.14.refs_3_, ...), custom_call_target="tpu_custom_call" | custom-call | tf_op jit(solution)/shard_map/contract/pallas_call | solution.py:336
  93.4 1.8 %collective-permute-done.20.refs_7_ = bf16[160,384]{1,0:T(8,128)(2,1)S(1)} collective-permute-done((bf16[160,384]{1,0:T(8,128)(2,1)S(1)}, bf16[160,384]{1,0:T(8,128)(2,1)S(1)}, u32[]{:S(2)}, u32[]{:S(2)}) %collective-permute-start.20) | collective-permute-done | bytes 122912 | tf_op jit(solution)/shard_map/ppermute | solution.py:449
  95.2 0.9 contract.3
  96.7 1.0 collective-permute-done.25.refs_4_
  98.3 1.7 %collective-permute-start.26 = (bf16[64,1408]{1,0:T(8,128)(2,1)S(1)}, bf16[64,1408]{1,0:T(8,128)(2,1)S(1)}, u32[]{:S(2)}, u32[]{:S(2)}) collective-permute-start(bf16[64,1408]{1,0:T(8,128)(2,1)S(1)} %get-tuple-element.153), channel_id=1, source_target_pairs={{0,8},{8,0},{16,24},{24,16},{1,9},{9,1},{17,25},{25,17},{2,10},{10... | collective-permute-start | bytes 540680 | tf_op jit(solution)/shard_map/ppermute | solution.py:454
  100.0 2.6 %collective-permute-start.27 = (bf16[64,1408]{1,0:T(8,128)(2,1)S(1)}, bf16[64,1408]{1,0:T(8,128)(2,1)S(1)}, u32[]{:S(2)}, u32[]{:S(2)}) collective-permute-start(bf16[64,1408]{1,0:T(8,128)(2,1)S(1)} %get-tuple-element.154), channel_id=1, source_target_pairs={{0,16},{8,24},{16,0},{24,8},{1,17},{9,25},{17,1},{25,9},{2,18},{10... | collective-permute-start | bytes 540680 | tf_op jit(solution)/shard_map/ppermute | solution.py:454
  102.8 5.8 %collective-permute-done.26.refs_3_ = bf16[64,1408]{1,0:T(8,128)(2,1)S(1)} collective-permute-done((bf16[64,1408]{1,0:T(8,128)(2,1)S(1)}, bf16[64,1408]{1,0:T(8,128)(2,1)S(1)}, u32[]{:S(2)}, u32[]{:S(2)}) %collective-permute-start.26) | collective-permute-done | bytes 180256 | tf_op jit(solution)/shard_map/ppermute | solution.py:454
  108.6 7.5 %collective-permute-done.27.refs_4_ = bf16[64,1408]{1,0:T(8,128)(2,1)S(1)} collective-permute-done((bf16[64,1408]{1,0:T(8,128)(2,1)S(1)}, bf16[64,1408]{1,0:T(8,128)(2,1)S(1)}, u32[]{:S(2)}, u32[]{:S(2)}) %collective-permute-start.27) | collective-permute-done | bytes 180256 | tf_op jit(solution)/shard_map/ppermute | solution.py:454
  116.0 1.4 %finish.1 = (f32[32,288]{1,0:T(8,128)}, f32[4,72]{1,0:T(4,128)}, f32[1,64]{1,0:T(1,128)}, f32[64,1024]{1,0:T(8,128)}) custom-call(s32[5]{0:T(128)S(1)} %stack.23.refs_0_, f32[64,1024]{1,0:T(8,128)S(1)} %get-tuple-element.151.refs_1_, f32[64,384]{1,0:T(8,128)S(1)} %get-tuple-element.152.refs_2_, bf16[64,1408]{1,0:T(8,128)(2,1)S(1)} %collective-permute-done.26.refs_3_, ...), custom_call_target="tpu_custom_call" | custom-call | tf_op jit(solution)/shard_map/finish/pallas_call | solution.py:430
  (60 shorter events, 10.3 us)
Async XLA Ops:
  0.6 20.5 %collective-permute-start.2 = (bf16[128,4096]{1,0:T(8,128)(2,1)}, bf16[128,4096]{1,0:T(8,128)(2,1)}, u32[]{:S(2)}, u32[]{:S(2)}) collective-permute-start(bf16[128,4096]{1,0:T(8,128)(2,1)} %bitcast.19), channel_id=1, source_target_pairs={{0,1},{1,0},{2,3},{3,2},{4,5},{5,4},{6,7},{7,6},{8,9},{9,8},{10,11... | collective-permute-start | bytes 3145736 | tf_op jit(solution)/shard_map/ppermute | solution.py:444
  1.2 27.6 %collective-permute-start = (bf16[128,4096]{1,0:T(8,128)(2,1)}, bf16[128,4096]{1,0:T(8,128)(2,1)S(1)}, u32[]{:S(2)}, u32[]{:S(2)}) collective-permute-start(bf16[128,4096]{1,0:T(8,128)(2,1)} %bitcast.20), channel_id=1, source_target_pairs={{0,2},{1,3},{2,0},{3,1},{4,6},{5,7},{6,4},{7,5},{8,10},{9,11},{10,... | collective-permute-start | bytes 3145736 | tf_op jit(solution)/shard_map/ppermute | solution.py:449
  3.7 25.5 %collective-permute-start.1 = (bf16[128,4096]{1,0:T(8,128)(2,1)}, bf16[128,4096]{1,0:T(8,128)(2,1)}, u32[]{:S(2)}, u32[]{:S(2)}) collective-permute-start(bf16[128,4096]{1,0:T(8,128)(2,1)} %bitcast.21), channel_id=1, source_target_pairs={{0,4},{1,5},{2,6},{3,7},{4,0},{5,1},{6,2},{7,3},{8,12},{9,13},{10,... | collective-permute-start | bytes 3145736 | tf_op jit(solution)/shard_map/ppermute | solution.py:449
  29.3 4.1 %collective-permute-start.6 = (bf16[128,4096]{1,0:T(8,128)(2,1)S(1)}, bf16[128,4096]{1,0:T(8,128)(2,1)S(1)}, u32[]{:S(2)}, u32[]{:S(2)}) collective-permute-start(bf16[128,4096]{1,0:T(8,128)(2,1)S(1)} %collective-permute-done.refs_1_), channel_id=1, source_target_pairs={{0,1},{1,0},{2,3},{3,2},{4,5},{5,4},{6,7},{7,6},{8,9},{9,8},{10,11... | collective-permute-start | bytes 3145736 | tf_op jit(solution)/shard_map/ppermute | solution.py:444
  29.3 4.4 %collective-permute-start.7 = (bf16[128,4096]{1,0:T(8,128)(2,1)}, bf16[128,4096]{1,0:T(8,128)(2,1)S(1)}, u32[]{:S(2)}, u32[]{:S(2)}) collective-permute-start(bf16[128,4096]{1,0:T(8,128)(2,1)} %collective-permute-done.1.refs_2_), channel_id=1, source_target_pairs={{0,1},{1,0},{2,3},{3,2},{4,5},{5,4},{6,7},{7,6},{8,9},{9,8},{10,11... | collective-permute-start | bytes 3145736 | tf_op jit(solution)/shard_map/ppermute | solution.py:444
  30.9 15.8 %collective-permute-start.4 = (bf16[64,4096]{1,0:T(8,128)(2,1)S(1)}, bf16[64,4096]{1,0:T(8,128)(2,1)S(1)}, u32[]{:S(2)}, u32[]{:S(2)}) collective-permute-start(bf16[64,4096]{1,0:T(8,128)(2,1)S(1)} %slice.14), channel_id=1, source_target_pairs={{0,2},{1,3},{2,0},{3,1},{4,6},{5,7},{6,4},{7,5},{8,10},{9,11},{10,... | collective-permute-start | bytes 1572872 | tf_op jit(solution)/shard_map/ppermute | solution.py:449
  31.3 15.4 %collective-permute-start.5 = (bf16[64,4096]{1,0:T(8,128)(2,1)S(1)}, bf16[64,4096]{1,0:T(8,128)(2,1)S(1)}, u32[]{:S(2)}, u32[]{:S(2)}) collective-permute-start(bf16[64,4096]{1,0:T(8,128)(2,1)S(1)} %slice.15), channel_id=1, source_target_pairs={{0,4},{1,5},{2,6},{3,7},{4,0},{5,1},{6,2},{7,3},{8,12},{9,13},{10,... | collective-permute-start | bytes 1572872 | tf_op jit(solution)/shard_map/ppermute | solution.py:449
  46.8 2.8 %collective-permute-start.11 = (bf16[64,4096]{1,0:T(8,128)(2,1)S(1)}, bf16[64,4096]{1,0:T(8,128)(2,1)S(1)}, u32[]{:S(2)}, u32[]{:S(2)}) collective-permute-start(bf16[64,4096]{1,0:T(8,128)(2,1)S(1)} %collective-permute-done.4.refs_1_), channel_id=1, source_target_pairs={{0,1},{1,0},{2,3},{3,2},{4,5},{5,4},{6,7},{7,6},{8,9},{9,8},{10,11... | collective-permute-start | bytes 1572872 | tf_op jit(solution)/shard_map/ppermute | solution.py:444
  47.0 4.0 %collective-permute-start.12 = (bf16[64,4096]{1,0:T(8,128)(2,1)S(1)}, bf16[64,4096]{1,0:T(8,128)(2,1)S(1)}, u32[]{:S(2)}, u32[]{:S(2)}) collective-permute-start(bf16[64,4096]{1,0:T(8,128)(2,1)S(1)} %collective-permute-done.5.refs_2_), channel_id=1, source_target_pairs={{0,1},{1,0},{2,3},{3,2},{4,5},{5,4},{6,7},{7,6},{8,9},{9,8},{10,11... | collective-permute-start | bytes 1572872 | tf_op jit(solution)/shard_map/ppermute | solution.py:444
  47.3 12.5 %collective-permute-start.8 = (bf16[256,1024]{1,0:T(8,128)(2,1)S(1)}, bf16[256,1024]{1,0:T(8,128)(2,1)S(1)}, u32[]{:S(2)}, u32[]{:S(2)}) collective-permute-start(bf16[256,1024]{1,0:T(8,128)(2,1)S(1)} %get-tuple-element.108), channel_id=1, source_target_pairs={{0,1},{1,0},{2,3},{3,2},{4,5},{5,4},{6,7},{7,6},{8,9},{9,8},{10,11... | collective-permute-start | bytes 1572872 | tf_op jit(solution)/shard_map/ppermute | solution.py:444
  47.5 10.8 %collective-permute-start.13 = (bf16[128,768]{1,0:T(8,128)(2,1)S(1)}, bf16[128,768]{1,0:T(8,128)(2,1)S(1)}, u32[]{:S(2)}, u32[]{:S(2)}) collective-permute-start(bf16[128,768]{1,0:T(8,128)(2,1)S(1)} %get-tuple-element.114), channel_id=1, source_target_pairs={{0,2},{1,3},{2,0},{3,1},{4,6},{5,7},{6,4},{7,5},{8,10},{9,11},{10,... | collective-permute-start | bytes 589832 | tf_op jit(solution)/shard_map/ppermute | solution.py:449
  48.3 10.0 %collective-permute-start.14 = (bf16[128,768]{1,0:T(8,128)(2,1)S(1)}, bf16[128,768]{1,0:T(8,128)(2,1)S(1)}, u32[]{:S(2)}, u32[]{:S(2)}) collective-permute-start(bf16[128,768]{1,0:T(8,128)(2,1)S(1)} %get-tuple-element.115), channel_id=1, source_target_pairs={{0,4},{1,5},{2,6},{3,7},{4,0},{5,1},{6,2},{7,3},{8,12},{9,13},{10,... | collective-permute-start | bytes 589832 | tf_op jit(solution)/shard_map/ppermute | solution.py:449
  49.6 10.3 %collective-permute-start.15 = (bf16[128,768]{1,0:T(8,128)(2,1)S(1)}, bf16[128,768]{1,0:T(8,128)(2,1)S(1)}, u32[]{:S(2)}, u32[]{:S(2)}) collective-permute-start(bf16[128,768]{1,0:T(8,128)(2,1)S(1)} %get-tuple-element.116), channel_id=1, source_target_pairs={{0,6},{1,7},{2,4},{3,5},{4,2},{5,3},{6,0},{7,1},{8,14},{9,15},{10,... | collective-permute-start | bytes 589832 | tf_op jit(solution)/shard_map/ppermute | solution.py:449
  51.0 13.0 %collective-permute-start.3 = (bf16[128,1024]{1,0:T(8,128)(2,1)S(1)}, bf16[128,1024]{1,0:T(8,128)(2,1)S(1)}, u32[]{:S(2)}, u32[]{:S(2)}) collective-permute-start(bf16[128,1024]{1,0:T(8,128)(2,1)S(1)} %get-tuple-element.98), channel_id=1, source_target_pairs={{0,1},{1,0},{2,3},{3,2},{4,5},{5,4},{6,7},{7,6},{8,9},{9,8},{10,11... | collective-permute-start | bytes 786440 | tf_op jit(solution)/shard_map/ppermute | solution.py:444
  58.2 21.4 %copy-start.3 = (f32[4,2304]{1,0:T(4,128)S(1)}, f32[4,2304]{1,0:T(4,128)}, u32[]{:S(2)}) copy-start(f32[4,2304]{1,0:T(4,128)} %conv_w.1) | copy-start | bytes 110596
  58.3 21.4 %copy-start.5 = (f32[2048]{0:T(1024)S(1)}, f32[2048]{0:T(1024)}, u32[]{:S(2)}) copy-start(f32[2048]{0:T(1024)} %param.38) | copy-start | bytes 24580
  59.8 2.8 %collective-permute-start.16 = (bf16[128,1024]{1,0:T(8,128)(2,1)S(1)}, bf16[128,1024]{1,0:T(8,128)(2,1)S(1)}, u32[]{:S(2)}, u32[]{:S(2)}) collective-permute-start(bf16[128,1024]{1,0:T(8,128)(2,1)S(1)} %get-tuple-element.118), channel_id=1, source_target_pairs={{0,1},{1,0},{2,3},{3,2},{4,5},{5,4},{6,7},{7,6},{8,9},{9,8},{10,11... | collective-permute-start | bytes 786440 | tf_op jit(solution)/shard_map/ppermute | solution.py:444
  60.3 8.8 %collective-permute-start.10 = (bf16[128,1024]{1,0:T(8,128)(2,1)S(1)}, bf16[128,1024]{1,0:T(8,128)(2,1)S(1)}, u32[]{:S(2)}, u32[]{:S(2)}) collective-permute-start(bf16[128,1024]{1,0:T(8,128)(2,1)S(1)} %get-tuple-element.161), channel_id=1, source_target_pairs={{0,4},{1,5},{2,6},{3,7},{4,0},{5,1},{6,2},{7,3},{8,12},{9,13},{10,... | collective-permute-start | bytes 786440 | tf_op jit(solution)/shard_map/ppermute | solution.py:449
  61.2 9.1 %collective-permute-start.9 = (bf16[128,1024]{1,0:T(8,128)(2,1)S(1)}, bf16[128,1024]{1,0:T(8,128)(2,1)S(1)}, u32[]{:S(2)}, u32[]{:S(2)}) collective-permute-start(bf16[128,1024]{1,0:T(8,128)(2,1)S(1)} %get-tuple-element.160), channel_id=1, source_target_pairs={{0,2},{1,3},{2,0},{3,1},{4,6},{5,7},{6,4},{7,5},{8,10},{9,11},{10,... | collective-permute-start | bytes 786440 | tf_op jit(solution)/shard_map/ppermute | solution.py:449
  62.7 13.1 %collective-permute-start.17 = (bf16[128,1024]{1,0:T(8,128)(2,1)S(1)}, bf16[128,1024]{1,0:T(8,128)(2,1)S(1)}, u32[]{:S(2)}, u32[]{:S(2)}) collective-permute-start(bf16[128,1024]{1,0:T(8,128)(2,1)S(1)} %add_convert_fusion.1), channel_id=1, source_target_pairs={{0,6},{1,7},{2,4},{3,5},{4,2},{5,3},{6,0},{7,1},{8,14},{9,15},{10,... | collective-permute-start | bytes 786440 | tf_op jit(solution)/shard_map/ppermute | solution.py:449
  76.1 10.3 %collective-permute-start.18 = (bf16[128,1024]{1,0:T(8,128)(2,1)S(1)}, bf16[128,1024]{1,0:T(8,128)(2,1)S(1)}, u32[]{:S(2)}, u32[]{:S(2)}) collective-permute-start(bf16[128,1024]{1,0:T(8,128)(2,1)S(1)} %multiply_convert_fusion.d_out.refs_5_), channel_id=1, source_target_pairs={{0,2},{1,3},{2,0},{3,1},{4,6},{5,7},{6,4},{7,5},{8,10},{9,11},{10,... | collective-permute-start | bytes 786440 | tf_op jit(solution)/shard_map/ppermute | solution.py:449
  77.0 13.0 %collective-permute-start.22 = (bf16[128,1024]{1,0:T(8,128)(2,1)S(1)}, bf16[128,1024]{1,0:T(8,128)(2,1)S(1)}, u32[]{:S(2)}, u32[]{:S(2)}) collective-permute-start(bf16[128,1024]{1,0:T(8,128)(2,1)S(1)} %multiply_convert_fusion.d_out.refs_5_), channel_id=1, source_target_pairs={{0,4},{1,5},{2,6},{3,7},{4,0},{5,1},{6,2},{7,3},{8,12},{9,13},{10,... | collective-permute-start | bytes 786440 | tf_op jit(solution)/shard_map/ppermute | solution.py:449
  78.5 12.9 %collective-permute-start.23 = (bf16[128,1024]{1,0:T(8,128)(2,1)S(1)}, bf16[128,1024]{1,0:T(8,128)(2,1)S(1)}, u32[]{:S(2)}, u32[]{:S(2)}) collective-permute-start(bf16[128,1024]{1,0:T(8,128)(2,1)S(1)} %multiply_convert_fusion.d_out.refs_5_), channel_id=1, source_target_pairs={{0,6},{1,7},{2,4},{3,5},{4,2},{5,3},{6,0},{7,1},{8,14},{9,15},{10,... | collective-permute-start | bytes 786440 | tf_op jit(solution)/shard_map/ppermute | solution.py:449
  79.7 37.8 %copy-start.1 = (bf16[1024,1024]{1,0:T(8,128)(2,1)S(1)}, bf16[1024,1024]{1,0:T(8,128)(2,1)}, u32[]{:S(2)}) copy-start(bf16[1024,1024]{1,0:T(8,128)(2,1)} %param.28) | copy-start | bytes 6291460
  86.4 7.0 %collective-permute-start.19 = (bf16[160,384]{1,0:T(8,128)(2,1)S(1)}, bf16[160,384]{1,0:T(8,128)(2,1)S(1)}, u32[]{:S(2)}, u32[]{:S(2)}) collective-permute-start(bf16[160,384]{1,0:T(8,128)(2,1)S(1)} %student_backward.1.refs_5_), channel_id=1, source_target_pairs={{0,2},{1,3},{2,0},{3,1},{4,6},{5,7},{6,4},{7,5},{8,10},{9,11},{10,... | collective-permute-start | bytes 368648 | tf_op jit(solution)/shard_map/ppermute | solution.py:449
  87.3 7.9 %collective-permute-start.20 = (bf16[160,384]{1,0:T(8,128)(2,1)S(1)}, bf16[160,384]{1,0:T(8,128)(2,1)S(1)}, u32[]{:S(2)}, u32[]{:S(2)}) collective-permute-start(bf16[160,384]{1,0:T(8,128)(2,1)S(1)} %student_backward.1.refs_5_), channel_id=1, source_target_pairs={{0,4},{1,5},{2,6},{3,7},{4,0},{5,1},{6,2},{7,3},{8,12},{9,13},{10,... | collective-permute-start | bytes 368648 | tf_op jit(solution)/shard_map/ppermute | solution.py:449
  88.8 6.4 %collective-permute-start.21 = (bf16[160,384]{1,0:T(8,128)(2,1)S(1)}, bf16[160,384]{1,0:T(8,128)(2,1)S(1)}, u32[]{:S(2)}, u32[]{:S(2)}) collective-permute-start(bf16[160,384]{1,0:T(8,128)(2,1)S(1)} %student_backward.1.refs_5_), channel_id=1, source_target_pairs={{0,6},{1,7},{2,4},{3,5},{4,2},{5,3},{6,0},{7,1},{8,14},{9,15},{10,... | collective-permute-start | bytes 368648 | tf_op jit(solution)/shard_map/ppermute | solution.py:449
  95.2 2.5 %collective-permute-start.24 = (bf16[256,1024]{1,0:T(8,128)(2,1)S(1)}, bf16[256,1024]{1,0:T(8,128)(2,1)S(1)}, u32[]{:S(2)}, u32[]{:S(2)}) collective-permute-start(bf16[256,1024]{1,0:T(8,128)(2,1)S(1)} %get-tuple-element.144), channel_id=1, source_target_pairs={{0,1},{1,0},{2,3},{3,2},{4,5},{5,4},{6,7},{7,6},{8,9},{9,8},{10,11... | collective-permute-start | bytes 1572872 | tf_op jit(solution)/shard_map/ppermute | solution.py:444
  96.1 1.5 %collective-permute-start.25 = (bf16[160,384]{1,0:T(8,128)(2,1)S(1)}, bf16[160,384]{1,0:T(8,128)(2,1)S(1)}, u32[]{:S(2)}, u32[]{:S(2)}) collective-permute-start(bf16[160,384]{1,0:T(8,128)(2,1)S(1)} %get-tuple-element.150), channel_id=1, source_target_pairs={{0,1},{1,0},{2,3},{3,2},{4,5},{5,4},{6,7},{7,6},{8,9},{9,8},{10,11... | collective-permute-start | bytes 368648 | tf_op jit(solution)/shard_map/ppermute | solution.py:444
  98.3 10.2 %collective-permute-start.26 = (bf16[64,1408]{1,0:T(8,128)(2,1)S(1)}, bf16[64,1408]{1,0:T(8,128)(2,1)S(1)}, u32[]{:S(2)}, u32[]{:S(2)}) collective-permute-start(bf16[64,1408]{1,0:T(8,128)(2,1)S(1)} %get-tuple-element.153), channel_id=1, source_target_pairs={{0,8},{8,0},{16,24},{24,16},{1,9},{9,1},{17,25},{25,17},{2,10},{10... | collective-permute-start | bytes 540680 | tf_op jit(solution)/shard_map/ppermute | solution.py:454
  100.0 16.1 %collective-permute-start.27 = (bf16[64,1408]{1,0:T(8,128)(2,1)S(1)}, bf16[64,1408]{1,0:T(8,128)(2,1)S(1)}, u32[]{:S(2)}, u32[]{:S(2)}) collective-permute-start(bf16[64,1408]{1,0:T(8,128)(2,1)S(1)} %get-tuple-element.154), channel_id=1, source_target_pairs={{0,16},{8,24},{16,0},{24,8},{1,17},{9,25},{17,1},{25,9},{2,18},{10... | collective-permute-start | bytes 540680 | tf_op jit(solution)/shard_map/ppermute | solution.py:454
  102.6 13.5 %collective-permute-start.28 = (bf16[64,1408]{1,0:T(8,128)(2,1)S(1)}, bf16[64,1408]{1,0:T(8,128)(2,1)S(1)}, u32[]{:S(2)}, u32[]{:S(2)}) collective-permute-start(bf16[64,1408]{1,0:T(8,128)(2,1)S(1)} %get-tuple-element.155), channel_id=1, source_target_pairs={{0,24},{8,16},{16,8},{24,0},{1,25},{9,17},{17,9},{25,1},{2,26},{10... | collective-permute-start | bytes 540680 | tf_op jit(solution)/shard_map/ppermute | solution.py:454
  (5 other events, 76.0 us)

commit v2 on v1

--- a/solution.py
+++ b/solution.py
@@ -506,6 +506,32 @@
     )(meta, *pieces, teacher_gain.reshape(1, width), *in_vmem([w_gate, w_up, readout, proj]))
 
 
+def cut_kernel(half, first, second, top, bottom, sems):
+    copies = [
+        pltpu.make_async_copy(first.at[pl.ds(0, half), :], top, sems.at[0]),
+        pltpu.make_async_copy(second.at[pl.ds(half, half), :], bottom, sems.at[1]),
+    ]
+    for copy in copies:
+        copy.start()
+    for copy in copies:
+        copy.wait()
+
+
+def halves_to_forward(first, second, half):
+    kind = jax.ShapeDtypeStruct((half, first.shape[1]), first.dtype)
+    anywhere = pl.BlockSpec(memory_space=pl.ANY)
+    return pl.pallas_call(
+        lambda *refs: cut_kernel(half, *refs),
+        name="cut",
+        in_specs=[anywhere, anywhere],
+        out_specs=[anywhere, anywhere],
+        out_shape=[kind, kind],
+        scratch_shapes=[pltpu.SemaphoreType.DMA((2,))],
+        compiler_params=pltpu.CompilerParams(vmem_limit_bytes=1 << 20),
+        cost_estimate=NO_COST,
+    )(first, second)
+
+
 def per_device(
     teacher_in, teacher_gain, w_gate, w_up, readout, distill_proj, building_ids, student_in,
     embed_rows, covariates, cov_proj, student_gain, w_x, w_bcdt, conv_w, dt_bias, a_log, d_skip,
@@ -555,7 +581,8 @@
 
     if chips == 4:
         half = seq_len // 2
-        corner = [hop(across[1][:half], 1), hop(across[0][half:], 2)]
+        top, bottom = halves_to_forward(across[1], across[0], half)
+        corner = [hop(top, 1), hop(bottom, 2)]
         second = teach(across)
         corner, second, cols = lax.optimization_barrier((corner, second, cols))
         parts = settle(first, (0,)) + settle(second, (1, 2))

time: 118 us -> 118 us (level)
  local copies, waits for them, and re-layouts: 3.3 us -> 1.97 us
  transfers between devices with their start and end apart: 29 -> 29, of which waited for: 13 -> 13; matrix products, arithmetic and copies ran while one was open for 3% -> 2% of each run, Pallas kernels for 43% -> 44%
where the time goes in v2:
time: 118 us; the launch traced here: 117 us
  Pallas kernels  53.4 us (45%)
  waiting for transfers between devices  32.5 us (28%)
  starting transfers between devices  27.2 us (23%)
  local copies, waits for them, and re-layouts  1.97 us (2%)
  between operations  1.54 us (1%)
    pallas_call x3, Pallas kernels, teacher_terms(): pl.pallas_call(lambda *refs: teacher_kernel(len(pieces), *refs), name='te...  28 us
    ppermute x16, starting transfers between devices, hop(): lax.ppermute(values, 'head', [(i, i ^ 2 * step) for i in range(size)])  20.4 us
    ppermute x16, waiting for transfers between devices, hop(): lax.ppermute(values, 'head', [(i, i ^ 2 * step) for i in range(size)])  17.5 us
    pallas_call x1, Pallas kernels, student_forward(): pl.pallas_call(lambda *refs: forward_kernel(chips, levels, *refs), name='...  13.3 us
    ppermute x3, waiting for transfers between devices, level(): return lax.ppermute(values, 'series', [(i, i ^ step) for i in range(size)])  13.3 us
    pallas_call x1, Pallas kernels, student_backward(): pl.pallas_call(backward_kernel, name='student_backward', in_specs=[VMEM]...  6.7 us
    ppermute x3, starting transfers between devices, level(): return lax.ppermute(values, 'series', [(i, i ^ step) for i in range(size)])  4.47 us
  transfers between devices with their start and end apart: 29, of which 13 were waited for; matrix products, arithmetic and copies ran while one was open for 2% of the time, Pallas kernels for 44%

profile of v2, /device:TPU:0, one launch (start us, length us, event | category | flops | bytes accessed | tf_op | source)
XLA Modules:
  0.0 117.0 jit_solution(11848107198295545745)
XLA Ops:
  1.2 2.6 %collective-permute-start = (bf16[128,4096]{1,0:T(8,128)(2,1)}, bf16[128,4096]{1,0:T(8,128)(2,1)S(1)}, u32[]{:S(2)}, u32[]{:S(2)}) collective-permute-start(bf16[128,4096]{1,0:T(8,128)(2,1)} %bitcast.20), channel_id=1, source_target_pairs={{0,2},{1,3},{2,0},{3,1},{4,6},{5,7},{6,4},{7,5},{8,10},{9,11},{10,... | collective-permute-start | bytes 3145736 | tf_op jit(solution)/shard_map/ppermute | solution.py:449
  3.7 1.5 %collective-permute-start.1 = (bf16[128,4096]{1,0:T(8,128)(2,1)}, bf16[128,4096]{1,0:T(8,128)(2,1)}, u32[]{:S(2)}, u32[]{:S(2)}) collective-permute-start(bf16[128,4096]{1,0:T(8,128)(2,1)} %bitcast.21), channel_id=1, source_target_pairs={{0,4},{1,5},{2,6},{3,7},{4,0},{5,1},{6,2},{7,3},{8,12},{9,13},{10,... | collective-permute-start | bytes 3145736 | tf_op jit(solution)/shard_map/ppermute | solution.py:449
  6.0 1.2 %constant_dynamic-slice_fusion.refs_3_ = bf16[1,128]{1,0:T(2,128)(2,1)} fusion(bf16[1024,128]{1,0:T(8,128)(2,1)} %param.29, s32[]{:T(128)S(6)} %select_n.17), kind=kLoop, calls=%fused_computation.3 | loop fusion | bytes 516 | tf_op jit(solution)/shard_map/dynamic_slice | solution.py:552
  7.8 13.3 %student_forward.1 = (bf16[2048,1024]{1,0:T(8,128)(2,1)S(1)}, bf16[4096,1024]{1,0:T(8,128)(2,1)S(1)}, bf16[4096,1024]{1,0:T(8,128)(2,1)S(1)}, bf16[1024,1024]{1,...) custom-call(s32[5]{0:T(128)S(1)} %stack.23.refs_0_, ...), custom_call_target="tpu_custom_call" | custom-call | tf_op jit(solution)/shard_map/student_forward/pallas_call | solution.py:269
  21.1 7.6 %teacher.3 = (f32[128,1024]{1,0:T(8,128)S(1)}, bf16[128,1024]{1,0:T(8,128)(2,1)S(1)}) custom-call(s32[5]{0:T(128)S(1)} %stack.23.refs_0_, bf16[128,4096]{1,0:T(8,128)(2,1)S(1)} %bitcast.22, bf16[128,4096]{1,0:T(8,128)(2,1)} %collective-permute-done.2.refs_2_, f32[1,4096]{1,0:T(1,128)S(1)} %bitcast.23, ...), custom_call_target="tpu_custom_call" | custom-call | tf_op jit(solution)/shard_map/teacher/pallas_call | solution.py:491
  29.8 1.1 cut.1
  31.3 1.7 %collective-permute-start.5 = (bf16[64,4096]{1,0:T(8,128)(2,1)S(1)}, bf16[64,4096]{1,0:T(8,128)(2,1)S(1)}, u32[]{:S(2)}, u32[]{:S(2)}) collective-permute-start(bf16[64,4096]{1,0:T(8,128)(2,1)S(1)} %get-tuple-element.104), channel_id=1, source_target_pairs={{0,4},{1,5},{2,6},{3,7},{4,0},{5,1},{6,2},{7,3},{8,12},{9,13},{10,... | collective-permute-start | bytes 1572872 | tf_op jit(solution)/shard_map/ppermute | solution.py:449
  33.6 12.9 %teacher.4 = (f32[256,1024]{1,0:T(8,128)S(1)}, bf16[256,1024]{1,0:T(8,128)(2,1)S(1)}) custom-call(s32[5]{0:T(128)S(1)} %stack.23.refs_0_, bf16[128,4096]{1,0:T(8,128)(2,1)S(1)} %collective-permute-done.refs_1_, bf16[128,4096]{1,0:T(8,128)(2,1)} %collective-permute-done.1.refs_0_.refs_2_, bf16[128,4096]{1,0:T(8,128)(2,1)S(1)} %collective-permute-done.6.refs_3_, ...), custom_call_target="tpu_custom_call" | custom-call | tf_op jit(solution)/shard_map/teacher/pallas_call | solution.py:491
  48.1 1.3 %collective-permute-start.14 = (bf16[128,768]{1,0:T(8,128)(2,1)S(1)}, bf16[128,768]{1,0:T(8,128)(2,1)S(1)}, u32[]{:S(2)}, u32[]{:S(2)}) collective-permute-start(bf16[128,768]{1,0:T(8,128)(2,1)S(1)} %get-tuple-element.119), channel_id=1, source_target_pairs={{0,4},{1,5},{2,6},{3,7},{4,0},{5,1},{6,2},{7,3},{8,12},{9,13},{10,... | collective-permute-start | bytes 589832 | tf_op jit(solution)/shard_map/ppermute | solution.py:449
  49.4 1.4 %collective-permute-start.15 = (bf16[128,768]{1,0:T(8,128)(2,1)S(1)}, bf16[128,768]{1,0:T(8,128)(2,1)S(1)}, u32[]{:S(2)}, u32[]{:S(2)}) collective-permute-start(bf16[128,768]{1,0:T(8,128)(2,1)S(1)} %get-tuple-element.120), channel_id=1, source_target_pairs={{0,6},{1,7},{2,4},{3,5},{4,2},{5,3},{6,0},{7,1},{8,14},{9,15},{10,... | collective-permute-start | bytes 589832 | tf_op jit(solution)/shard_map/ppermute | solution.py:449
  50.8 7.5 %teacher.5 = (f32[128,1024]{1,0:T(8,128)S(1)}, bf16[128,1024]{1,0:T(8,128)(2,1)S(1)}) custom-call(s32[5]{0:T(128)S(1)} %stack.23.refs_0_, bf16[64,4096]{1,0:T(8,128)(2,1)S(1)} %collective-permute-done.4.refs_1_, bf16[64,4096]{1,0:T(8,128)(2,1)S(1)} %collective-permute-done.5.refs_2_, bf16[64,4096]{1,0:T(8,128)(2,1)S(1)} %collective-permute-done.11.refs_3_, ...), custom_call_target="tpu_custom_call" | custom-call | tf_op jit(solution)/shard_map/teacher/pallas_call | solution.py:491
  58.4 1.3 %collective-permute-done.15.refs_4_ = bf16[128,768]{1,0:T(8,128)(2,1)S(1)} collective-permute-done((bf16[128,768]{1,0:T(8,128)(2,1)S(1)}, bf16[128,768]{1,0:T(8,128)(2,1)S(1)}, u32[]{:S(2)}, u32[]{:S(2)}) %collective-permute-start.15) | collective-permute-done | bytes 196640 | tf_op jit(solution)/shard_map/ppermute | solution.py:449
  59.8 0.9 collective-permute-start.10
  60.7 1.5 %collective-permute-start.9 = (bf16[128,1024]{1,0:T(8,128)(2,1)S(1)}, bf16[128,1024]{1,0:T(8,128)(2,1)S(1)}, u32[]{:S(2)}, u32[]{:S(2)}) collective-permute-start(bf16[128,1024]{1,0:T(8,128)(2,1)S(1)} %get-tuple-element.164), channel_id=1, source_target_pairs={{0,2},{1,3},{2,0},{3,1},{4,6},{5,7},{6,4},{7,5},{8,10},{9,11},{10,... | collective-permute-start | bytes 786440 | tf_op jit(solution)/shard_map/ppermute | solution.py:449
  62.3 1.2 %collective-permute-start.17 = (bf16[128,1024]{1,0:T(8,128)(2,1)S(1)}, bf16[128,1024]{1,0:T(8,128)(2,1)S(1)}, u32[]{:S(2)}, u32[]{:S(2)}) collective-permute-start(bf16[128,1024]{1,0:T(8,128)(2,1)S(1)} %add_convert_fusion.1), channel_id=1, source_target_pairs={{0,6},{1,7},{2,4},{3,5},{4,2},{5,3},{6,0},{7,1},{8,14},{9,15},{10,... | collective-permute-start | bytes 786440 | tf_op jit(solution)/shard_map/ppermute | solution.py:449
  63.5 5.1 %collective-permute-done.10 = bf16[128,1024]{1,0:T(8,128)(2,1)S(1)} collective-permute-done((bf16[128,1024]{1,0:T(8,128)(2,1)S(1)}, bf16[128,1024]{1,0:T(8,128)(2,1)S(1)}, u32[]{:S(2)}, u32[]{:S(2)}) %collective-permute-start.10) | collective-permute-done | bytes 262176 | tf_op jit(solution)/shard_map/ppermute | solution.py:449
  68.6 1.3 %collective-permute-done.9 = bf16[128,1024]{1,0:T(8,128)(2,1)S(1)} collective-permute-done((bf16[128,1024]{1,0:T(8,128)(2,1)S(1)}, bf16[128,1024]{1,0:T(8,128)(2,1)S(1)}, u32[]{:S(2)}, u32[]{:S(2)}) %collective-permute-start.9) | collective-permute-done | bytes 262176 | tf_op jit(solution)/shard_map/ppermute | solution.py:449
  69.9 5.5 %collective-permute-done.17 = bf16[128,1024]{1,0:T(8,128)(2,1)S(1)} collective-permute-done((bf16[128,1024]{1,0:T(8,128)(2,1)S(1)}, bf16[128,1024]{1,0:T(8,128)(2,1)S(1)}, u32[]{:S(2)}, u32[]{:S(2)}) %collective-permute-start.17) | collective-permute-done | bytes 262176 | tf_op jit(solution)/shard_map/ppermute | solution.py:449
  76.5 1.5 %collective-permute-start.22 = (bf16[128,1024]{1,0:T(8,128)(2,1)S(1)}, bf16[128,1024]{1,0:T(8,128)(2,1)S(1)}, u32[]{:S(2)}, u32[]{:S(2)}) collective-permute-start(bf16[128,1024]{1,0:T(8,128)(2,1)S(1)} %multiply_convert_fusion.d_out.refs_5_), channel_id=1, source_target_pairs={{0,4},{1,5},{2,6},{3,7},{4,0},{5,1},{6,2},{7,3},{8,12},{9,13},{10,... | collective-permute-start | bytes 786440 | tf_op jit(solution)/shard_map/ppermute | solution.py:449
  78.0 1.2 %collective-permute-start.23 = (bf16[128,1024]{1,0:T(8,128)(2,1)S(1)}, bf16[128,1024]{1,0:T(8,128)(2,1)S(1)}, u32[]{:S(2)}, u32[]{:S(2)}) collective-permute-start(bf16[128,1024]{1,0:T(8,128)(2,1)S(1)} %multiply_convert_fusion.d_out.refs_5_), channel_id=1, source_target_pairs={{0,6},{1,7},{2,4},{3,5},{4,2},{5,3},{6,0},{7,1},{8,14},{9,15},{10,... | collective-permute-start | bytes 786440 | tf_op jit(solution)/shard_map/ppermute | solution.py:449
  79.2 6.7 %student_backward.1.refs_5_ = bf16[160,384]{1,0:T(8,128)(2,1)S(1)} custom-call(bf16[128,1024]{1,0:T(8,128)(2,1)S(1)} %multiply_convert_fusion.d_out.refs_5_, bf16[2048,1024]{1,0:T(8,128)(2,1)S(1)} %get-tuple-element.123.w_out, f32[1,2048]{1,0:T(1,128)S(1)} %bitcast.27, f32[4,2304]{1,0:T(4,128)S(1)} %copy-done.3, f32[1,32]{1,0:T(1,128)S(1)} %bitcast.29, ...), custom_call_target="tpu_custom_call" | custom-call | tf_op jit(solution)/shard_map/student_backward/pallas_call | solution.py:293
  86.8 1.5 %collective-permute-start.20 = (bf16[160,384]{1,0:T(8,128)(2,1)S(1)}, bf16[160,384]{1,0:T(8,128)(2,1)S(1)}, u32[]{:S(2)}, u32[]{:S(2)}) collective-permute-start(bf16[160,384]{1,0:T(8,128)(2,1)S(1)} %student_backward.1.refs_5_), channel_id=1, source_target_pairs={{0,4},{1,5},{2,6},{3,7},{4,0},{5,1},{6,2},{7,3},{8,12},{9,13},{10,... | collective-permute-start | bytes 368648 | tf_op jit(solution)/shard_map/ppermute | solution.py:449
  88.3 1.2 %collective-permute-start.21 = (bf16[160,384]{1,0:T(8,128)(2,1)S(1)}, bf16[160,384]{1,0:T(8,128)(2,1)S(1)}, u32[]{:S(2)}, u32[]{:S(2)}) collective-permute-start(bf16[160,384]{1,0:T(8,128)(2,1)S(1)} %student_backward.1.refs_5_), channel_id=1, source_target_pairs={{0,6},{1,7},{2,4},{3,5},{4,2},{5,3},{6,0},{7,1},{8,14},{9,15},{10,... | collective-permute-start | bytes 368648 | tf_op jit(solution)/shard_map/ppermute | solution.py:449
  89.5 1.4 %collective-permute-done.23.refs_8_ = bf16[128,1024]{1,0:T(8,128)(2,1)S(1)} collective-permute-done((bf16[128,1024]{1,0:T(8,128)(2,1)S(1)}, bf16[128,1024]{1,0:T(8,128)(2,1)S(1)}, u32[]{:S(2)}, u32[]{:S(2)}) %collective-permute-start.23) | collective-permute-done | bytes 262176 | tf_op jit(solution)/shard_map/ppermute | solution.py:449
  91.0 1.4 %contract.2 = (f32[256,1024]{1,0:T(8,128)S(1)}, bf16[256,1024]{1,0:T(8,128)(2,1)S(1)}) custom-call(s32[5]{0:T(128)S(1)} %stack.23.refs_0_, bf16[128,768]{1,0:T(8,128)(2,1)S(1)} %get-tuple-element.140.refs_1_, bf16[128,768]{1,0:T(8,128)(2,1)S(1)} %collective-permute-done.13.refs_2_, bf16[128,768]{1,0:T(8,128)(2,1)S(1)} %collective-permute-done.14.refs_3_, ...), custom_call_target="tpu_custom_call" | custom-call | tf_op jit(solution)/shard_map/contract/pallas_call | solution.py:336
  93.0 1.8 %collective-permute-done.20.refs_7_ = bf16[160,384]{1,0:T(8,128)(2,1)S(1)} collective-permute-done((bf16[160,384]{1,0:T(8,128)(2,1)S(1)}, bf16[160,384]{1,0:T(8,128)(2,1)S(1)}, u32[]{:S(2)}, u32[]{:S(2)}) %collective-permute-start.20) | collective-permute-done | bytes 122912 | tf_op jit(solution)/shard_map/ppermute | solution.py:449
  96.2 1.0 collective-permute-done.25.refs_4_
  97.9 1.7 %collective-permute-start.26 = (bf16[64,1408]{1,0:T(8,128)(2,1)S(1)}, bf16[64,1408]{1,0:T(8,128)(2,1)S(1)}, u32[]{:S(2)}, u32[]{:S(2)}) collective-permute-start(bf16[64,1408]{1,0:T(8,128)(2,1)S(1)} %get-tuple-element.157), channel_id=1, source_target_pairs={{0,8},{8,0},{16,24},{24,16},{1,9},{9,1},{17,25},{25,17},{2,10},{10... | collective-permute-start | bytes 540680 | tf_op jit(solution)/shard_map/ppermute | solution.py:454
  99.5 2.6 %collective-permute-start.27 = (bf16[64,1408]{1,0:T(8,128)(2,1)S(1)}, bf16[64,1408]{1,0:T(8,128)(2,1)S(1)}, u32[]{:S(2)}, u32[]{:S(2)}) collective-permute-start(bf16[64,1408]{1,0:T(8,128)(2,1)S(1)} %get-tuple-element.158), channel_id=1, source_target_pairs={{0,16},{8,24},{16,0},{24,8},{1,17},{9,25},{17,1},{25,9},{2,18},{10... | collective-permute-start | bytes 540680 | tf_op jit(solution)/shard_map/ppermute | solution.py:454
  102.3 5.8 %collective-permute-done.26.refs_3_ = bf16[64,1408]{1,0:T(8,128)(2,1)S(1)} collective-permute-done((bf16[64,1408]{1,0:T(8,128)(2,1)S(1)}, bf16[64,1408]{1,0:T(8,128)(2,1)S(1)}, u32[]{:S(2)}, u32[]{:S(2)}) %collective-permute-start.26) | collective-permute-done | bytes 180256 | tf_op jit(solution)/shard_map/ppermute | solution.py:454
  108.1 7.5 %collective-permute-done.27.refs_4_ = bf16[64,1408]{1,0:T(8,128)(2,1)S(1)} collective-permute-done((bf16[64,1408]{1,0:T(8,128)(2,1)S(1)}, bf16[64,1408]{1,0:T(8,128)(2,1)S(1)}, u32[]{:S(2)}, u32[]{:S(2)}) %collective-permute-start.27) | collective-permute-done | bytes 180256 | tf_op jit(solution)/shard_map/ppermute | solution.py:454
  115.6 1.4 %finish.1 = (f32[32,288]{1,0:T(8,128)}, f32[4,72]{1,0:T(4,128)}, f32[1,64]{1,0:T(1,128)}, f32[64,1024]{1,0:T(8,128)}) custom-call(s32[5]{0:T(128)S(1)} %stack.23.refs_0_, f32[64,1024]{1,0:T(8,128)S(1)} %get-tuple-element.155.refs_1_, f32[64,384]{1,0:T(8,128)S(1)} %get-tuple-element.156.refs_2_, bf16[64,1408]{1,0:T(8,128)(2,1)S(1)} %collective-permute-done.26.refs_3_, ...), custom_call_target="tpu_custom_call" | custom-call | tf_op jit(solution)/shard_map/finish/pallas_call | solution.py:430
  (59 shorter events, 10.1 us)
Async XLA Ops:
  0.6 20.5 %collective-permute-start.2 = (bf16[128,4096]{1,0:T(8,128)(2,1)}, bf16[128,4096]{1,0:T(8,128)(2,1)}, u32[]{:S(2)}, u32[]{:S(2)}) collective-permute-start(bf16[128,4096]{1,0:T(8,128)(2,1)} %bitcast.19), channel_id=1, source_target_pairs={{0,1},{1,0},{2,3},{3,2},{4,5},{5,4},{6,7},{7,6},{8,9},{9,8},{10,11... | collective-permute-start | bytes 3145736 | tf_op jit(solution)/shard_map/ppermute | solution.py:444
  1.2 27.6 %collective-permute-start = (bf16[128,4096]{1,0:T(8,128)(2,1)}, bf16[128,4096]{1,0:T(8,128)(2,1)S(1)}, u32[]{:S(2)}, u32[]{:S(2)}) collective-permute-start(bf16[128,4096]{1,0:T(8,128)(2,1)} %bitcast.20), channel_id=1, source_target_pairs={{0,2},{1,3},{2,0},{3,1},{4,6},{5,7},{6,4},{7,5},{8,10},{9,11},{10,... | collective-permute-start | bytes 3145736 | tf_op jit(solution)/shard_map/ppermute | solution.py:449
  3.7 25.5 %collective-permute-start.1 = (bf16[128,4096]{1,0:T(8,128)(2,1)}, bf16[128,4096]{1,0:T(8,128)(2,1)}, u32[]{:S(2)}, u32[]{:S(2)}) collective-permute-start(bf16[128,4096]{1,0:T(8,128)(2,1)} %bitcast.21), channel_id=1, source_target_pairs={{0,4},{1,5},{2,6},{3,7},{4,0},{5,1},{6,2},{7,3},{8,12},{9,13},{10,... | collective-permute-start | bytes 3145736 | tf_op jit(solution)/shard_map/ppermute | solution.py:449
  29.3 4.1 %collective-permute-start.6 = (bf16[128,4096]{1,0:T(8,128)(2,1)S(1)}, bf16[128,4096]{1,0:T(8,128)(2,1)S(1)}, u32[]{:S(2)}, u32[]{:S(2)}) collective-permute-start(bf16[128,4096]{1,0:T(8,128)(2,1)S(1)} %collective-permute-done.refs_1_), channel_id=1, source_target_pairs={{0,1},{1,0},{2,3},{3,2},{4,5},{5,4},{6,7},{7,6},{8,9},{9,8},{10,11... | collective-permute-start | bytes 3145736 | tf_op jit(solution)/shard_map/ppermute | solution.py:444
  29.3 4.4 %collective-permute-start.7 = (bf16[128,4096]{1,0:T(8,128)(2,1)}, bf16[128,4096]{1,0:T(8,128)(2,1)S(1)}, u32[]{:S(2)}, u32[]{:S(2)}) collective-permute-start(bf16[128,4096]{1,0:T(8,128)(2,1)} %collective-permute-done.1.refs_0_.refs_2_), channel_id=1, source_target_pairs={{0,1},{1,0},{2,3},{3,2},{4,5},{5,4},{6,7},{7,6},{8,9},{9,8},{10,11... | collective-permute-start | bytes 3145736 | tf_op jit(solution)/shard_map/ppermute | solution.py:444
  30.9 15.7 %collective-permute-start.4 = (bf16[64,4096]{1,0:T(8,128)(2,1)S(1)}, bf16[64,4096]{1,0:T(8,128)(2,1)S(1)}, u32[]{:S(2)}, u32[]{:S(2)}) collective-permute-start(bf16[64,4096]{1,0:T(8,128)(2,1)S(1)} %get-tuple-element.103), channel_id=1, source_target_pairs={{0,2},{1,3},{2,0},{3,1},{4,6},{5,7},{6,4},{7,5},{8,10},{9,11},{10,... | collective-permute-start | bytes 1572872 | tf_op jit(solution)/shard_map/ppermute | solution.py:449
  31.3 15.3 %collective-permute-start.5 = (bf16[64,4096]{1,0:T(8,128)(2,1)S(1)}, bf16[64,4096]{1,0:T(8,128)(2,1)S(1)}, u32[]{:S(2)}, u32[]{:S(2)}) collective-permute-start(bf16[64,4096]{1,0:T(8,128)(2,1)S(1)} %get-tuple-element.104), channel_id=1, source_target_pairs={{0,4},{1,5},{2,6},{3,7},{4,0},{5,1},{6,2},{7,3},{8,12},{9,13},{10,... | collective-permute-start | bytes 1572872 | tf_op jit(solution)/shard_map/ppermute | solution.py:449
  46.6 2.8 %collective-permute-start.11 = (bf16[64,4096]{1,0:T(8,128)(2,1)S(1)}, bf16[64,4096]{1,0:T(8,128)(2,1)S(1)}, u32[]{:S(2)}, u32[]{:S(2)}) collective-permute-start(bf16[64,4096]{1,0:T(8,128)(2,1)S(1)} %collective-permute-done.4.refs_1_), channel_id=1, source_target_pairs={{0,1},{1,0},{2,3},{3,2},{4,5},{5,4},{6,7},{7,6},{8,9},{9,8},{10,11... | collective-permute-start | bytes 1572872 | tf_op jit(solution)/shard_map/ppermute | solution.py:444
  46.8 4.0 %collective-permute-start.12 = (bf16[64,4096]{1,0:T(8,128)(2,1)S(1)}, bf16[64,4096]{1,0:T(8,128)(2,1)S(1)}, u32[]{:S(2)}, u32[]{:S(2)}) collective-permute-start(bf16[64,4096]{1,0:T(8,128)(2,1)S(1)} %collective-permute-done.5.refs_2_), channel_id=1, source_target_pairs={{0,1},{1,0},{2,3},{3,2},{4,5},{5,4},{6,7},{7,6},{8,9},{9,8},{10,11... | collective-permute-start | bytes 1572872 | tf_op jit(solution)/shard_map/ppermute | solution.py:444
  47.1 12.5 %collective-permute-start.8 = (bf16[256,1024]{1,0:T(8,128)(2,1)S(1)}, bf16[256,1024]{1,0:T(8,128)(2,1)S(1)}, u32[]{:S(2)}, u32[]{:S(2)}) collective-permute-start(bf16[256,1024]{1,0:T(8,128)(2,1)S(1)} %get-tuple-element.112), channel_id=1, source_target_pairs={{0,1},{1,0},{2,3},{3,2},{4,5},{5,4},{6,7},{7,6},{8,9},{9,8},{10,11... | collective-permute-start | bytes 1572872 | tf_op jit(solution)/shard_map/ppermute | solution.py:444
  47.3 11.0 %collective-permute-start.13 = (bf16[128,768]{1,0:T(8,128)(2,1)S(1)}, bf16[128,768]{1,0:T(8,128)(2,1)S(1)}, u32[]{:S(2)}, u32[]{:S(2)}) collective-permute-start(bf16[128,768]{1,0:T(8,128)(2,1)S(1)} %get-tuple-element.118), channel_id=1, source_target_pairs={{0,2},{1,3},{2,0},{3,1},{4,6},{5,7},{6,4},{7,5},{8,10},{9,11},{10,... | collective-permute-start | bytes 589832 | tf_op jit(solution)/shard_map/ppermute | solution.py:449
  48.1 10.3 %collective-permute-start.14 = (bf16[128,768]{1,0:T(8,128)(2,1)S(1)}, bf16[128,768]{1,0:T(8,128)(2,1)S(1)}, u32[]{:S(2)}, u32[]{:S(2)}) collective-permute-start(bf16[128,768]{1,0:T(8,128)(2,1)S(1)} %get-tuple-element.119), channel_id=1, source_target_pairs={{0,4},{1,5},{2,6},{3,7},{4,0},{5,1},{6,2},{7,3},{8,12},{9,13},{10,... | collective-permute-start | bytes 589832 | tf_op jit(solution)/shard_map/ppermute | solution.py:449
  49.4 10.3 %collective-permute-start.15 = (bf16[128,768]{1,0:T(8,128)(2,1)S(1)}, bf16[128,768]{1,0:T(8,128)(2,1)S(1)}, u32[]{:S(2)}, u32[]{:S(2)}) collective-permute-start(bf16[128,768]{1,0:T(8,128)(2,1)S(1)} %get-tuple-element.120), channel_id=1, source_target_pairs={{0,6},{1,7},{2,4},{3,5},{4,2},{5,3},{6,0},{7,1},{8,14},{9,15},{10,... | collective-permute-start | bytes 589832 | tf_op jit(solution)/shard_map/ppermute | solution.py:449
  50.8 12.7 %collective-permute-start.3 = (bf16[128,1024]{1,0:T(8,128)(2,1)S(1)}, bf16[128,1024]{1,0:T(8,128)(2,1)S(1)}, u32[]{:S(2)}, u32[]{:S(2)}) collective-permute-start(bf16[128,1024]{1,0:T(8,128)(2,1)S(1)} %get-tuple-element.100), channel_id=1, source_target_pairs={{0,1},{1,0},{2,3},{3,2},{4,5},{5,4},{6,7},{7,6},{8,9},{9,8},{10,11... | collective-permute-start | bytes 786440 | tf_op jit(solution)/shard_map/ppermute | solution.py:444
  58.3 20.9 %copy-start.3 = (f32[4,2304]{1,0:T(4,128)S(1)}, f32[4,2304]{1,0:T(4,128)}, u32[]{:S(2)}) copy-start(f32[4,2304]{1,0:T(4,128)} %conv_w.1) | copy-start | bytes 110596
  58.3 20.9 %copy-start.5 = (f32[2048]{0:T(1024)S(1)}, f32[2048]{0:T(1024)}, u32[]{:S(2)}) copy-start(f32[2048]{0:T(1024)} %param.38) | copy-start | bytes 24580
  59.6 2.6 %collective-permute-start.16 = (bf16[128,1024]{1,0:T(8,128)(2,1)S(1)}, bf16[128,1024]{1,0:T(8,128)(2,1)S(1)}, u32[]{:S(2)}, u32[]{:S(2)}) collective-permute-start(bf16[128,1024]{1,0:T(8,128)(2,1)S(1)} %get-tuple-element.122), channel_id=1, source_target_pairs={{0,1},{1,0},{2,3},{3,2},{4,5},{5,4},{6,7},{7,6},{8,9},{9,8},{10,11... | collective-permute-start | bytes 786440 | tf_op jit(solution)/shard_map/ppermute | solution.py:444
  59.8 8.8 %collective-permute-start.10 = (bf16[128,1024]{1,0:T(8,128)(2,1)S(1)}, bf16[128,1024]{1,0:T(8,128)(2,1)S(1)}, u32[]{:S(2)}, u32[]{:S(2)}) collective-permute-start(bf16[128,1024]{1,0:T(8,128)(2,1)S(1)} %get-tuple-element.165), channel_id=1, source_target_pairs={{0,4},{1,5},{2,6},{3,7},{4,0},{5,1},{6,2},{7,3},{8,12},{9,13},{10,... | collective-permute-start | bytes 786440 | tf_op jit(solution)/shard_map/ppermute | solution.py:449
  60.7 9.1 %collective-permute-start.9 = (bf16[128,1024]{1,0:T(8,128)(2,1)S(1)}, bf16[128,1024]{1,0:T(8,128)(2,1)S(1)}, u32[]{:S(2)}, u32[]{:S(2)}) collective-permute-start(bf16[128,1024]{1,0:T(8,128)(2,1)S(1)} %get-tuple-element.164), channel_id=1, source_target_pairs={{0,2},{1,3},{2,0},{3,1},{4,6},{5,7},{6,4},{7,5},{8,10},{9,11},{10,... | collective-permute-start | bytes 786440 | tf_op jit(solution)/shard_map/ppermute | solution.py:449
  62.3 13.1 %collective-permute-start.17 = (bf16[128,1024]{1,0:T(8,128)(2,1)S(1)}, bf16[128,1024]{1,0:T(8,128)(2,1)S(1)}, u32[]{:S(2)}, u32[]{:S(2)}) collective-permute-start(bf16[128,1024]{1,0:T(8,128)(2,1)S(1)} %add_convert_fusion.1), channel_id=1, source_target_pairs={{0,6},{1,7},{2,4},{3,5},{4,2},{5,3},{6,0},{7,1},{8,14},{9,15},{10,... | collective-permute-start | bytes 786440 | tf_op jit(solution)/shard_map/ppermute | solution.py:449
  75.7 10.3 %collective-permute-start.18 = (bf16[128,1024]{1,0:T(8,128)(2,1)S(1)}, bf16[128,1024]{1,0:T(8,128)(2,1)S(1)}, u32[]{:S(2)}, u32[]{:S(2)}) collective-permute-start(bf16[128,1024]{1,0:T(8,128)(2,1)S(1)} %multiply_convert_fusion.d_out.refs_5_), channel_id=1, source_target_pairs={{0,2},{1,3},{2,0},{3,1},{4,6},{5,7},{6,4},{7,5},{8,10},{9,11},{10,... | collective-permute-start | bytes 786440 | tf_op jit(solution)/shard_map/ppermute | solution.py:449
  76.5 13.0 %collective-permute-start.22 = (bf16[128,1024]{1,0:T(8,128)(2,1)S(1)}, bf16[128,1024]{1,0:T(8,128)(2,1)S(1)}, u32[]{:S(2)}, u32[]{:S(2)}) collective-permute-start(bf16[128,1024]{1,0:T(8,128)(2,1)S(1)} %multiply_convert_fusion.d_out.refs_5_), channel_id=1, source_target_pairs={{0,4},{1,5},{2,6},{3,7},{4,0},{5,1},{6,2},{7,3},{8,12},{9,13},{10,... | collective-permute-start | bytes 786440 | tf_op jit(solution)/shard_map/ppermute | solution.py:449
  78.0 12.9 %collective-permute-start.23 = (bf16[128,1024]{1,0:T(8,128)(2,1)S(1)}, bf16[128,1024]{1,0:T(8,128)(2,1)S(1)}, u32[]{:S(2)}, u32[]{:S(2)}) collective-permute-start(bf16[128,1024]{1,0:T(8,128)(2,1)S(1)} %multiply_convert_fusion.d_out.refs_5_), channel_id=1, source_target_pairs={{0,6},{1,7},{2,4},{3,5},{4,2},{5,3},{6,0},{7,1},{8,14},{9,15},{10,... | collective-permute-start | bytes 786440 | tf_op jit(solution)/shard_map/ppermute | solution.py:449
  79.2 37.8 %copy-start.1 = (bf16[1024,1024]{1,0:T(8,128)(2,1)S(1)}, bf16[1024,1024]{1,0:T(8,128)(2,1)}, u32[]{:S(2)}) copy-start(bf16[1024,1024]{1,0:T(8,128)(2,1)} %param.28) | copy-start | bytes 6291460
  86.0 7.0 %collective-permute-start.19 = (bf16[160,384]{1,0:T(8,128)(2,1)S(1)}, bf16[160,384]{1,0:T(8,128)(2,1)S(1)}, u32[]{:S(2)}, u32[]{:S(2)}) collective-permute-start(bf16[160,384]{1,0:T(8,128)(2,1)S(1)} %student_backward.1.refs_5_), channel_id=1, source_target_pairs={{0,2},{1,3},{2,0},{3,1},{4,6},{5,7},{6,4},{7,5},{8,10},{9,11},{10,... | collective-permute-start | bytes 368648 | tf_op jit(solution)/shard_map/ppermute | solution.py:449
  86.8 7.9 %collective-permute-start.20 = (bf16[160,384]{1,0:T(8,128)(2,1)S(1)}, bf16[160,384]{1,0:T(8,128)(2,1)S(1)}, u32[]{:S(2)}, u32[]{:S(2)}) collective-permute-start(bf16[160,384]{1,0:T(8,128)(2,1)S(1)} %student_backward.1.refs_5_), channel_id=1, source_target_pairs={{0,4},{1,5},{2,6},{3,7},{4,0},{5,1},{6,2},{7,3},{8,12},{9,13},{10,... | collective-permute-start | bytes 368648 | tf_op jit(solution)/shard_map/ppermute | solution.py:449
  88.3 6.4 %collective-permute-start.21 = (bf16[160,384]{1,0:T(8,128)(2,1)S(1)}, bf16[160,384]{1,0:T(8,128)(2,1)S(1)}, u32[]{:S(2)}, u32[]{:S(2)}) collective-permute-start(bf16[160,384]{1,0:T(8,128)(2,1)S(1)} %student_backward.1.refs_5_), channel_id=1, source_target_pairs={{0,6},{1,7},{2,4},{3,5},{4,2},{5,3},{6,0},{7,1},{8,14},{9,15},{10,... | collective-permute-start | bytes 368648 | tf_op jit(solution)/shard_map/ppermute | solution.py:449
  94.8 2.5 %collective-permute-start.24 = (bf16[256,1024]{1,0:T(8,128)(2,1)S(1)}, bf16[256,1024]{1,0:T(8,128)(2,1)S(1)}, u32[]{:S(2)}, u32[]{:S(2)}) collective-permute-start(bf16[256,1024]{1,0:T(8,128)(2,1)S(1)} %get-tuple-element.148), channel_id=1, source_target_pairs={{0,1},{1,0},{2,3},{3,2},{4,5},{5,4},{6,7},{7,6},{8,9},{9,8},{10,11... | collective-permute-start | bytes 1572872 | tf_op jit(solution)/shard_map/ppermute | solution.py:444
  95.7 1.5 %collective-permute-start.25 = (bf16[160,384]{1,0:T(8,128)(2,1)S(1)}, bf16[160,384]{1,0:T(8,128)(2,1)S(1)}, u32[]{:S(2)}, u32[]{:S(2)}) collective-permute-start(bf16[160,384]{1,0:T(8,128)(2,1)S(1)} %get-tuple-element.154), channel_id=1, source_target_pairs={{0,1},{1,0},{2,3},{3,2},{4,5},{5,4},{6,7},{7,6},{8,9},{9,8},{10,11... | collective-permute-start | bytes 368648 | tf_op jit(solution)/shard_map/ppermute | solution.py:444
  97.9 10.2 %collective-permute-start.26 = (bf16[64,1408]{1,0:T(8,128)(2,1)S(1)}, bf16[64,1408]{1,0:T(8,128)(2,1)S(1)}, u32[]{:S(2)}, u32[]{:S(2)}) collective-permute-start(bf16[64,1408]{1,0:T(8,128)(2,1)S(1)} %get-tuple-element.157), channel_id=1, source_target_pairs={{0,8},{8,0},{16,24},{24,16},{1,9},{9,1},{17,25},{25,17},{2,10},{10... | collective-permute-start | bytes 540680 | tf_op jit(solution)/shard_map/ppermute | solution.py:454
  99.5 16.1 %collective-permute-start.27 = (bf16[64,1408]{1,0:T(8,128)(2,1)S(1)}, bf16[64,1408]{1,0:T(8,128)(2,1)S(1)}, u32[]{:S(2)}, u32[]{:S(2)}) collective-permute-start(bf16[64,1408]{1,0:T(8,128)(2,1)S(1)} %get-tuple-element.158), channel_id=1, source_target_pairs={{0,16},{8,24},{16,0},{24,8},{1,17},{9,25},{17,1},{25,9},{2,18},{10... | collective-permute-start | bytes 540680 | tf_op jit(solution)/shard_map/ppermute | solution.py:454
  102.1 13.5 %collective-permute-start.28 = (bf16[64,1408]{1,0:T(8,128)(2,1)S(1)}, bf16[64,1408]{1,0:T(8,128)(2,1)S(1)}, u32[]{:S(2)}, u32[]{:S(2)}) collective-permute-start(bf16[64,1408]{1,0:T(8,128)(2,1)S(1)} %get-tuple-element.159), channel_id=1, source_target_pairs={{0,24},{8,16},{16,8},{24,0},{1,25},{9,17},{17,9},{25,1},{2,26},{10... | collective-permute-start | bytes 540680 | tf_op jit(solution)/shard_map/ppermute | solution.py:454
  (5 other events, 75.0 us)
